TPU v7x, 512 devices: a whole 4x8x8 slice. The times are simulated.
512 devices in a mesh: sweep: 32 (over x, z_hi, core), span: 16 (over z_lo, y).
Axes of the slice: x: 4, y: 8, z: 8 (z_hi: 4, z_lo: 2; z = z_hi * 2 + z_lo), core: 2. Of those that a mesh axis runs over, the one named last changes fastest.
Arguments:
- inverses: bfloat16 [32, 16, 6, 135, 135], P('sweep', 'span')
- couplings: bfloat16 [6, 32, 16, 6, 135, 135], P(None, 'sweep', 'span')
- rhs: bfloat16 [32, 16, 6, 135, 128], P('sweep', 'span'), may hold values from -6 to 6
- previous: bfloat16 [32, 16, 6, 135, 128], P('sweep', 'span'), may hold values from -6 to 6
- slot_layer: int32 [32, 16, 6], P('sweep', 'span'), may hold values from 0 to 5, each once within a row
Outputs:
- solution: float32 [32, 16, 6, 135, 128], P('sweep', 'span')
Inputs may be any that keep to these rules, and one draw needn't show every extreme that they name: `slot_layer`: in each line each wall-normal layer is stored in exactly one slot.
All inputs are finite; a program needn't handle non-finite values.
Results may differ from a plain program's by a relative error of at most 0.0029.
Values may be sent and summed in bfloat16 or wider, within the bound.
No kernel may reach another device: no remote copies, remote signals or barrier semaphores. Data moves between devices by JAX's collectives and lax.ppermute only.
A program may use at most 128 MiB of HBM per device.

v0:
```python
import jax
import jax.numpy as jnp
from jax import lax
from jax.sharding import PartitionSpec as P


def padded_2(value, sides, width):
    for axis, dim in sides:
        devices, length = (lax.axis_size(axis), value.shape[dim])
        up = [(i, (i + 1) % devices) for i in range(devices)]
        down = [(j, i) for i, j in up]
        last = lax.slice_in_dim(value, length - width, length, axis=dim)
        initial = lax.slice_in_dim(value, 0, width, axis=dim)
        before = lax.ppermute(last, axis, up)
        after = lax.ppermute(initial, axis, down)
        value = jnp.concatenate([before, value, after], axis=dim)
    return value


def from_behind(block, axis, distance):
    devices = range(lax.axis_size(axis))
    route = [(i - distance, i) for i in devices if i - distance in devices]
    return lax.ppermute(block, axis, route)


def carried_in(value, axis, join, neutral):
    count, mine = (lax.axis_size(axis), lax.axis_index(axis))
    pieces = jax.tree.map(lambda part: lax.all_gather(part, axis), value)
    so_far = jax.tree.map(
        lambda part, zero: jnp.full_like(part, 0) + jnp.asarray(zero, part.dtype), value, neutral
    )

    def step(position, so_far):
        longer = join(so_far, jax.tree.map(lambda part: part[position], pieces))
        return jax.tree.map(lambda new, old: jnp.where(position < mine, new, old), longer, so_far)

    return lax.fori_loop(0, count - 1, step, so_far)


def couple(blocks, vectors):
    return jnp.einsum("plzab,plzbr->plzar", blocks, vectors, preferred_element_type=jnp.float32)


def apply_map(matrix, vectors):
    return jnp.einsum("lzab,lzbr->lzar", matrix, vectors, precision=lax.Precision.HIGHEST)


def compose(earlier, latter):
    return (apply_map(latter[0], earlier[0]), apply_map(latter[0], earlier[1]) + latter[1])


def select_layers(slot_layer, values, step_by):
    chooser = (slot_layer[:, :, None, :] == slot_layer[:, :, :, None] + step_by).astype(
        jnp.bfloat16
    )
    picked = jnp.einsum("plst,pltbr->plsbr", chooser, values, preferred_element_type=jnp.float32)
    return picked.astype(jnp.bfloat16)


def local(inverses, couplings, rhs, previous, slot_layer):
    padded = padded_2(previous, (("span", 1),), 1)
    span_lower = padded[:, :-2]
    span_upper = padded[:, 2:]
    beyond = from_behind(previous, "sweep", -1)
    downstream = jnp.concatenate([previous[1:], beyond], axis=0)
    wall_lower = select_layers(slot_layer, previous, -1)
    wall_upper = select_layers(slot_layer, previous, 1)
    transfer = -couple(inverses, couplings[0])
    coupled = couple(couplings[1], downstream)
    coupled = coupled + couple(couplings[2], span_lower)
    coupled = coupled + couple(couplings[3], span_upper)
    coupled = coupled + couple(couplings[4], wall_lower)
    coupled = coupled + couple(couplings[5], wall_upper)
    forcing = (rhs.astype(jnp.float32) - coupled).astype(jnp.bfloat16)
    offset = couple(inverses, forcing)
    own_matrix = transfer[0]
    own_shift = offset[0]
    width = transfer.shape[-1]
    unit_maps = jnp.broadcast_to(jnp.eye(width, dtype=jnp.float32), own_matrix.shape)
    identity = (unit_maps, jnp.zeros_like(own_shift))
    prefix = carried_in((own_matrix, own_shift), "sweep", compose, identity)
    current = prefix[1]
    current = offset[0] + apply_map(transfer[0], current)
    results = [current]
    solution = jnp.stack(results)
    return solution


def solution(mesh):
    return jax.shard_map(
        local,
        mesh=mesh,
        in_specs=(
            P("sweep", "span", None, None, None),
            P(None, "sweep", "span", None, None, None),
            P("sweep", "span", None, None, None),
            P("sweep", "span", None, None, None),
            P("sweep", "span", None),
        ),
        out_specs=P("sweep", "span", None, None, None),
        check_vma=False,
    )
```

profile of v0, /device:TPU:1, one launch (start us, length us, event | category | flops | bytes accessed | tf_op | source)
XLA Modules:
  0.0 395.8 jit_solution(18204895806765643080)
XLA Ops:
  6.5 0.0 copy-start
  6.5 0.0 copy-start.3
  6.5 0.0 all-gather.7.cloned.1.call-start
  6.5 8.0 %collective-permute-start.2 = (bf16[1,1,6,135,128]{4,3,2,1,0:T(8,128)(2,1)}, bf16[1,1,6,135,128]{4,3,2,1,0:T(8,128)(2,1)S(1)}, u32[]{:S(2)}, u32[]{:S(2)}) collective-permute-start(bf16[1,1,6,135,128]{4,3,2,1,0:T(8,128)(2,1)} %param.10), channel_id=1, source_target_pairs={{1,0},{2,1},{3,2},{4,3},{5,4},{6,5},{7,6},{8,7},{9,8},{10,9},{11,1... | collective-permute-start | bytes 622088 | tf_op jit(solution)/shard_map/ppermute | solution.py:15
  14.5 1.9 collective-permute-start.1
  16.5 4.9 %collective-permute-start = (bf16[1,1,6,135,128]{4,3,2,1,0:T(8,128)(2,1)}, bf16[1,1,6,135,128]{4,3,2,1,0:T(8,128)(2,1)}, u32[]{:S(2)}, u32[]{:S(2)}) collective-permute-start(bf16[1,1,6,135,128]{4,3,2,1,0:T(8,128)(2,1)} %param.10), channel_id=1, source_target_pairs={{16,0},{32,16},{48,32},{64,48},{80,64},{96,80},{112,96},{128,112},... | collective-permute-start | bytes 622088 | tf_op jit(solution)/shard_map/ppermute | solution.py:23
  21.4 0.7 broadcast_add_fusion.1
  22.1 0.0 copy-start.4
  22.1 1.3 fusion.38
  23.4 1.2 fusion.40
  24.6 1.3 convolution_bitcast_fusion.1
  25.9 2.0 convolution_bitcast_fusion.2
  27.9 0.0 collective-permute-done.2
  27.9 0.0 copy-done.3
  27.9 1.0 fusion.24
  28.9 0.0 collective-permute-done.1
  28.9 1.0 fusion.26
  30.0 0.0 collective-permute-done
  30.0 0.0 copy-done
  30.0 0.0 copy-done.4
  30.0 2.6 convolution_bitcast_fusion
  32.5 0.0 all-gather.7.cloned.1.call-update
  32.6 0.0 all-gather.5.cloned.1.call-start
  32.6 1.2 convolution_negate_fusion
  33.8 0.0 all-gather.5.cloned.1.call-update
  33.8 107.3 %all-gather.7.cloned.1.call-done = f32[192,135,128]{2,1,0:T(8,128)} async-done(((f32[6,135,128]{2,1,0:T(8,128)}), f32[192,135,128]{2,1,0:T(8,128)}) %all-gather.7.cloned.1.call-update) | async-done | bytes 13271056 | tf_op jit(solution)/shard_map/all_gather | solution.py:28
  141.1 176.5 %all-gather.5.cloned.1.call-done = f32[192,135,135]{2,1,0:T(8,128)} async-done(((f32[6,135,135]{2,1,0:T(8,128)}), f32[192,135,135]{2,1,0:T(8,128)}) %all-gather.5.cloned.1.call-update) | async-done | bytes 13996816 | tf_op jit(solution)/shard_map/all_gather | solution.py:28
  317.6 0.0 copy-start.1
  317.6 69.2 %while.14 = (s32[]{:T(128)}, f32[1,6,135,128]{3,2,1,0:T(8,128)S(1)}, s32[]{:T(128)}, f32[32,1,6,135,135]{4,3,2,1,0:T(8,128)}, f32[32,1,6,135,128]{4,3,2,1,0:T(8,128)}, /*index=5*/s32[]{:T(128)}, s32[]{:T(128)}) while((s32[]{:T(128)}, f32[1,6,135,128]{3,2,1,0:T(8,128)S(1)}, s32[]{:T(128)}, f32[32,1,6,135,135]{4,3,2,1,0:T(8,128)}, ...), condition=%wide.region_1.2_spmd.clone, body=%wide.region_0.1_spmd.clone.sunk | while | flops 168376320 | bytes 3335775 | solution.py:37
  317.7 2.3 fusion.60
  320.0 2.2 fusion.60
  322.2 2.2 fusion.60
  324.5 2.2 fusion.60
  326.7 2.2 fusion.60
  328.9 2.2 fusion.60
  331.2 2.2 fusion.60
  333.4 2.2 fusion.60
  335.6 2.2 fusion.60
  337.9 2.2 fusion.60
  340.1 2.2 fusion.60
  342.3 2.2 fusion.60
  344.6 2.2 fusion.60
  346.8 2.2 fusion.60
  349.0 2.2 fusion.60
  351.2 2.2 fusion.60
  353.5 2.2 fusion.60
  355.7 2.2 fusion.60
  357.9 2.2 fusion.60
  360.2 2.2 fusion.60
  362.4 2.2 fusion.60
  364.6 2.2 fusion.60
  366.9 2.2 fusion.60
  369.1 2.2 fusion.60
  371.3 2.2 fusion.60
  373.6 2.2 fusion.60
  375.8 2.2 fusion.60
  378.0 2.2 fusion.60
  380.3 2.2 fusion.60
  382.5 2.2 fusion.60
  384.7 2.2 fusion.60
  386.9 0.0 copy-done.1
  386.9 0.0 copy-done.2
  386.9 0.9 fusion.10
  387.8 1.2 copy.11
  (33 shorter events, 0.9 us)
Async XLA Ops:
  6.5 23.4 %copy-start = (bf16[1,1,6,135,135]{4,3,2,1,0:T(8,128)(2,1)S(1)}, bf16[1,1,6,135,135]{4,3,2,1,0:T(8,128)(2,1)}, u32[]{:S(2)}) copy-start(bf16[1,1,6,135,135]{4,3,2,1,0:T(8,128)(2,1)} %param.7) | copy-start | bytes 656104
  6.5 21.4 %copy-start.3 = (bf16[6,1,1,6,135,135]{5,4,3,2,1,0:T(8,128)(2,1)S(1)}, bf16[6,1,1,6,135,135]{5,4,3,2,1,0:T(8,128)(2,1)}, u32[]{:S(2)}) copy-start(bf16[6,1,1,6,135,135]{5,4,3,2,1,0:T(8,128)(2,1)} %param.8) | copy-start | bytes 3936604
  6.5 134.6 %all-gather.7.cloned.1.call-start = ((), (), s32[]{:S(2)}) async-start(), calls=%async_computation.1 | async-start | bytes 13787136 | tf_op jit(solution)/shard_map/all_gather | solution.py:28
  6.5 21.4 %collective-permute-start.2 = (bf16[1,1,6,135,128]{4,3,2,1,0:T(8,128)(2,1)}, bf16[1,1,6,135,128]{4,3,2,1,0:T(8,128)(2,1)S(1)}, u32[]{:S(2)}, u32[]{:S(2)}) collective-permute-start(bf16[1,1,6,135,128]{4,3,2,1,0:T(8,128)(2,1)} %param.10), channel_id=1, source_target_pairs={{1,0},{2,1},{3,2},{4,3},{5,4},{6,5},{7,6},{8,7},{9,8},{10,9},{11,1... | collective-permute-start | bytes 622088 | tf_op jit(solution)/shard_map/ppermute | solution.py:15
  14.5 14.4 %collective-permute-start.1 = (bf16[1,1,6,135,128]{4,3,2,1,0:T(8,128)(2,1)}, bf16[1,1,6,135,128]{4,3,2,1,0:T(8,128)(2,1)S(1)}, u32[]{:S(2)}, u32[]{:S(2)}) collective-permute-start(bf16[1,1,6,135,128]{4,3,2,1,0:T(8,128)(2,1)} %param.10), channel_id=1, source_target_pairs={{0,1},{1,2},{2,3},{3,4},{4,5},{5,6},{6,7},{7,8},{8,9},{9,10},{10,1... | collective-permute-start | bytes 622088 | tf_op jit(solution)/shard_map/ppermute | solution.py:14
  16.5 13.5 %collective-permute-start = (bf16[1,1,6,135,128]{4,3,2,1,0:T(8,128)(2,1)}, bf16[1,1,6,135,128]{4,3,2,1,0:T(8,128)(2,1)}, u32[]{:S(2)}, u32[]{:S(2)}) collective-permute-start(bf16[1,1,6,135,128]{4,3,2,1,0:T(8,128)(2,1)} %param.10), channel_id=1, source_target_pairs={{16,0},{32,16},{48,32},{64,48},{80,64},{96,80},{112,96},{128,112},... | collective-permute-start | bytes 622088 | tf_op jit(solution)/shard_map/ppermute | solution.py:23
  22.1 7.9 %copy-start.4 = (bf16[1,1,6,135,128]{4,3,2,1,0:T(8,128)(2,1)S(1)}, bf16[1,1,6,135,128]{4,3,2,1,0:T(8,128)(2,1)}, u32[]{:S(2)}) copy-start(bf16[1,1,6,135,128]{4,3,2,1,0:T(8,128)(2,1)} %param.9) | copy-start | bytes 622084
  32.6 285.1 %all-gather.5.cloned.1.call-start = ((), (), s32[]{:S(2)}) async-start(), calls=%async_computation | async-start | bytes 27574272 | tf_op jit(solution)/shard_map/all_gather | solution.py:28
  317.6 69.3 %copy-start.1 = (f32[6,135,135]{2,1,0:T(8,128)S(1)}, f32[6,135,135]{2,1,0:T(8,128)}, u32[]{:S(2)}) copy-start(f32[6,135,135]{2,1,0:T(8,128)} %convolution_negate_fusion) | copy-start | bytes 1312204
  317.6 69.3 %copy-start.2 = (f32[6,135,128]{2,1,0:T(8,128)S(1)}, f32[6,135,128]{2,1,0:T(8,128)}, u32[]{:S(2)}) copy-start(f32[6,135,128]{2,1,0:T(8,128)} %convolution_bitcast_fusion) | copy-start | bytes 1244164
Sparse Core Ops, SparseCore 0:
  32.7 108.4 all-gather.6
  144.3 173.3 all-gather.4
where the time goes:
time: 397 us; the launch traced here: 396 us
  waiting for transfers between devices  284 us (72%)
  matrix products  79.7 us (20%)
  starting transfers between devices  14.9 us (4%)
  between operations  13.5 us (3%)
    all_gather x2, waiting for transfers between devices, carried_in(): pieces = jax.tree.map(lambda part: lax.all_gather(part, axis), value)  284 us
    dot_general x32, matrix products, apply_map(): jnp.einsum('lzab,lzbr->lzar', matrix, vectors, precision=lax.Precision.HI...  68.1 us
    dot_general x6, matrix products, couple(): jnp.einsum('plzab,plzbr->plzar', blocks, vectors, preferred_element_type=...  9.09 us
    ppermute x1, starting transfers between devices, padded_2(): after = lax.ppermute(initial, axis, down)  7.98 us
  transfers between devices with their start and end apart: 5, of which 2 were waited for; matrix products, arithmetic and copies ran while one was open for 2% of the time, Pallas kernels for 0%

commit v1 on v0

v1 whole, which is shorter than its diff:
```python
import jax
import jax.numpy as jnp
from jax import lax
from jax.experimental import pallas as pl
from jax.experimental.pallas import tpu as pltpu
from jax.sharding import PartitionSpec as P

BS, NRHS, NZ = 135, 128, 6
ROWS = 136
LANE = 128
HALF = NZ // 2
NX_CHIPS, NZ_CHIPS = 4, 4
F32, BF16 = jnp.float32, jnp.bfloat16

SMEM = pl.BlockSpec(memory_space=pltpu.SMEM)
VMEM = pl.BlockSpec(memory_space=pltpu.VMEM)


def sweep_index(x, z, core):
    return (x * NZ_CHIPS + z) * 2 + core


Z_GROUPS = [[sweep_index(x, z, c) for z in range(NZ_CHIPS)] for x in range(NX_CHIPS) for c in range(2)]
X_GROUPS = [[sweep_index(x, z, c) for x in range(NX_CHIPS)] for z in range(NZ_CHIPS) for c in range(2)]


def face(index):
    return pl.BlockSpec((1, 1, 1, NZ, BS, BS), lambda i: (index, 0, 0, 0, 0, 0))


def mm(a, b):
    return jnp.dot(a, b, preferred_element_type=F32)


def split(v):
    hi = v.astype(BF16)
    return hi, (v - hi.astype(F32)).astype(BF16)


def mm3(a, b):
    return mm(a[0], b[0]) + (mm(a[0], b[1]) + mm(a[1], b[0]))


def pack(ref, at, main, tail, shift):
    r = main.shape[0]
    for place, value in ((0, main), (3, shift)):
        hi, lo = split(value)
        ref[at + (place, slice(0, r))] = hi
        ref[at + (place + 1, slice(0, r))] = lo
    hi, lo = split(tail)
    both = hi.astype(F32) + pltpu.roll(lo.astype(F32), 8, 1)
    ref[at + (2, slice(0, r))] = both.astype(BF16)


def unpack_tail(block):
    both = block.astype(F32)
    lane = lax.broadcasted_iota(jnp.int32, both.shape, 1)
    hi = jnp.where(lane < 8, both, 0.0)
    lo = jnp.where(lane < 8, pltpu.roll(both, LANE - 8, 1), 0.0)
    return hi, lo


def load_matrix(ref, at, scratch):
    tails = unpack_tail(ref[at + (2,)])
    for k in range(2):
        scratch[k, :, :LANE] = ref[at + (k,)]
        scratch[k, :, LANE:] = tails[k].astype(BF16)
    return scratch[0, :BS, :BS], scratch[1, :BS, :BS]


def load_shift(ref, at):
    return ref[at + (3, slice(0, BS))].astype(F32) + ref[at + (4, slice(0, BS))].astype(F32)


def transfer_kernel(inv, c0, out):
    for s in range(NZ):
        out[s] = -mm(inv[s], c0[0, 0, 0, s])


def wall_kernel(layers, c4, c5, rhs, prev, out):
    for s in range(NZ):
        layer = layers[s]
        total = rhs[s].astype(F32)
        for step, blocks in ((-1, c4), (1, c5)):
            found, exists = 0, 0
            for t in range(NZ):
                match = layers[t] == layer + step
                found = jnp.where(match, t, found)
                exists = jnp.where(match, 1, exists)
            keep = jnp.full((BS, NRHS), exists, jnp.int32) > 0
            vectors = jnp.where(keep, prev[found].astype(F32), 0.0).astype(BF16)
            total = total - mm(blocks[0, 0, 0, s], vectors)
        out[s] = total


def pair_kernel(core, own, sib, packed, second_out, final_out, scratch):
    c = core[0]
    scratch[...] = jnp.zeros_like(scratch)

    def body(first, second, mine):
        for s in range(NZ):
            t1 = split(second[s])
            second_out[s, 0], second_out[s, 1] = t1
            if mine == 0:
                final_out[s, 0], final_out[s, 1] = split(first[s])
                if s >= HALF:
                    continue
            a = mm3(t1, split(first[s]))
            if mine == 1:
                final_out[s, 0], final_out[s, 1] = split(a)
            if s // HALF == mine:
                scratch[:BS, :BS] = a
                for place, value in ((0, scratch[:, :LANE]),):
                    hi, lo = split(value)
                    packed[s % HALF, place] = hi
                    packed[s % HALF, place + 1] = lo
                hi, lo = split(scratch[:, LANE:])
                packed[s % HALF, 2] = (hi.astype(F32) + pltpu.roll(lo.astype(F32), 8, 1)).astype(BF16)

    pl.when(c == 0)(lambda: body(own, sib, 0))
    pl.when(c == 1)(lambda: body(sib, own, 1))


def offset_kernel(inv, c1, c2, c3, partial, down, lower, upper, out):
    for s in range(NZ):
        total = mm(c1[0, 0, 0, s], down[s]) + mm(c2[0, 0, 0, s], lower[s]) + mm(c3[0, 0, 0, s], upper[s])
        forcing = (partial[s] - total).astype(BF16)
        out[s] = mm(inv[s], forcing)


def send_kernel(core, second, own, sib, packed, send, shift_out):
    c = core[0]
    for s in range(HALF):
        send[s, 0:3] = packed[s]
    send[HALF] = jnp.zeros_like(send[HALF])

    def body(first_o, second_o, mine):
        for s in range(NZ):
            if mine == 0:
                shift_out[s] = first_o[s]
                if s >= HALF:
                    continue
            b = mm3((second[s, 0], second[s, 1]), split(first_o[s])) + second_o[s]
            if mine == 1:
                shift_out[s] = b
            if s // HALF == mine:
                send[s % HALF, 3, :BS], send[s % HALF, 4, :BS] = split(b)

    pl.when(c == 0)(lambda: body(own, sib, 0))
    pl.when(c == 1)(lambda: body(sib, own, 1))


def chain_kernel(recv, prefix, total, mat):
    tail = unpack_tail(recv[0, 2])
    main = recv[0, 0].astype(F32) + recv[0, 1].astype(F32)
    state = jnp.concatenate([main[:BS], load_shift(recv, (0,)), (tail[0] + tail[1])[:BS]], axis=1)
    for k in range(1, NZ_CHIPS + 1):
        if k > 1:
            fresh = mm3(load_matrix(recv, (k - 1,), mat), split(state))
            state = jnp.concatenate(
                [fresh[:, :LANE], fresh[:, LANE : 2 * LANE] + load_shift(recv, (k - 1,)), fresh[:, 2 * LANE :]], axis=1
            )
        parts = state[:, :LANE], state[:, 2 * LANE :], state[:, LANE : 2 * LANE]
        if k < NZ_CHIPS:
            pack(prefix, (k - 1,), *parts)
        else:
            for x in range(NX_CHIPS):
                pack(total, (x,), *parts)


def state_kernel(place, totals, prefix, send, state, mat):
    x = place[0]
    first = jnp.full((BS, NRHS), x, jnp.int32) > 0
    state[...] = jnp.where(first, load_shift(totals, (0,)), 0.0)
    for g in range(1, NX_CHIPS - 1):

        @pl.when(x > g)
        def _(g=g):
            state[...] = mm3(load_matrix(totals, (g,), mat), split(state[...])) + load_shift(totals, (g,))

    inflow = split(state[...])
    send[0, :BS] = inflow[0]
    for k in range(1, NZ_CHIPS):
        send[k, :BS] = (mm3(load_matrix(prefix, (k - 1,), mat), inflow) + load_shift(prefix, (k - 1,))).astype(BF16)


def final_kernel(core, matrix, shift, own, sib, out):
    c = core[0]

    def body(mine):
        for s in range(NZ):
            source = own if s // HALF == mine else sib
            v = source[s % HALF, :BS]
            out[s] = shift[s] + (mm(matrix[s, 0], v) + mm(matrix[s, 1], v))

    pl.when(c == 0)(lambda: body(0))
    pl.when(c == 1)(lambda: body(1))


def shape(*dims, dtype=F32):
    return jax.ShapeDtypeStruct(dims, dtype)


def call(kernel, outs, specs, scratch=(), **kw):
    single = not isinstance(outs, tuple)
    return pl.pallas_call(
        kernel,
        grid=(1,),
        out_shape=outs,
        in_specs=specs,
        out_specs=VMEM if single else (VMEM,) * len(outs),
        scratch_shapes=scratch,
        name=kernel.__name__,
        **kw,
    )


def local(inverses, couplings, rhs, previous, slot_layer):
    inv, rhs, prev, layers = inverses[0, 0], rhs[0, 0], previous[0, 0], slot_layer[0, 0]
    place = lax.axis_index("sweep")
    core = (place % 2).reshape(1).astype(jnp.int32)
    group = (place // (2 * NZ_CHIPS)).reshape(1).astype(jnp.int32)
    n_sweep, n_span = lax.axis_size("sweep"), lax.axis_size("span")
    swap = [(i, i ^ 1) for i in range(n_sweep)]

    lower = lax.ppermute(prev, "span", [(i, (i + 1) % n_span) for i in range(n_span)])
    upper = lax.ppermute(prev, "span", [((i + 1) % n_span, i) for i in range(n_span)])
    down = lax.ppermute(prev, "sweep", [(i + 1, i) for i in range(n_sweep - 1)])

    t_own = call(transfer_kernel, shape(NZ, BS, BS), [VMEM, face(0)])(inv, couplings)
    t_sib = lax.ppermute(t_own, "sweep", swap)
    partial = call(wall_kernel, shape(NZ, BS, NRHS), [SMEM, face(4), face(5), VMEM, VMEM])(layers, couplings, couplings, rhs, prev)
    packed, second, matrix = call(
        pair_kernel,
        (shape(HALF, 3, ROWS, LANE, dtype=BF16), shape(NZ, 2, BS, BS, dtype=BF16), shape(NZ, 2, BS, BS, dtype=BF16)),
        [SMEM, VMEM, VMEM],
        [pltpu.VMEM((ROWS, 2 * LANE), F32)],
    )(core, t_own, t_sib)
    o_own = call(offset_kernel, shape(NZ, BS, NRHS), [VMEM, face(1), face(2), face(3)] + [VMEM] * 4)(
        inv, couplings, couplings, couplings, partial, down, lower, upper
    )
    o_sib = lax.ppermute(o_own, "sweep", swap)
    send, shift = call(
        send_kernel, (shape(NZ_CHIPS, 5, ROWS, LANE, dtype=BF16), shape(NZ, BS, NRHS)), [SMEM] + [VMEM] * 4
    )(core, second, o_own, o_sib, packed)
    recv = lax.all_to_all(send, "sweep", 0, 0, axis_index_groups=Z_GROUPS)
    mat = pltpu.VMEM((2, ROWS, 2 * LANE), BF16)
    prefix, total = call(
        chain_kernel,
        (shape(NZ_CHIPS - 1, 5, ROWS, LANE, dtype=BF16), shape(NX_CHIPS, 5, ROWS, LANE, dtype=BF16)),
        [VMEM],
        [mat],
    )(recv)
    totals = lax.all_to_all(total, "sweep", 0, 0, axis_index_groups=X_GROUPS)
    back = call(
        state_kernel,
        shape(NZ_CHIPS, ROWS, NRHS, dtype=BF16),
        [SMEM, VMEM, VMEM],
        [pltpu.VMEM((BS, NRHS), F32), mat],
    )(group, totals, prefix)
    mine = lax.all_to_all(back, "sweep", 0, 0, axis_index_groups=Z_GROUPS)
    theirs = lax.ppermute(mine, "sweep", swap)
    out = call(final_kernel, shape(NZ, BS, NRHS), [SMEM] + [VMEM] * 4)(core, matrix, shift, mine, theirs)
    return out[None, None]


def solution(mesh):
    return jax.shard_map(
        local,
        mesh=mesh,
        in_specs=(
            P("sweep", "span", None, None, None),
            P(None, "sweep", "span", None, None, None),
            P("sweep", "span", None, None, None),
            P("sweep", "span", None, None, None),
            P("sweep", "span", None),
        ),
        out_specs=P("sweep", "span", None, None, None),
        check_vma=False,
    )
```

time: 397 us -> 109 us (0.27)
  waiting for transfers between devices: 284 us -> 8.84 us
  matrix products: 79.7 us -> 0 us
  blocking collectives: 0 us -> 37.4 us
  Pallas kernels: 0 us -> 23.2 us
  starting transfers between devices: 14.9 us -> 32.4 us
  between operations: 13.5 us -> 0.11 us
  local copies, waits for them, and re-layouts: 2.1 us -> 6.78 us
    all_gather x2 -> x0, waiting for transfers between devices: 284 us -> none  [carried_in(): pieces = jax.tree.map(lambda part: lax.all_gather(part, axis), value)]
    dot_general x40 -> x0, matrix products: 79.7 us -> none  [the longest x32 68.1 us: apply_map(): jnp.einsum('lzab,lzbr->lzar', matrix, vectors, precision=lax.Precision.HI...]
    all_to_all x0 -> x2, blocking collectives: none -> 37.4 us  [the longest x1 23.5 us: local(): recv = lax.all_to_all(send, 'sweep', 0, 0, axis_index_groups=Z_GROUPS)]
    pallas_call x0 -> x8, Pallas kernels: none -> 23.2 us  [the longest x1 4.19 us: local(): call(offset_kernel, shape(NZ, BS, NRHS), [VMEM, face(1), face(2), face(3)...]
    ppermute x3 -> x6, starting transfers between devices: 14.8 us -> 25.7 us  [the longest x1 8.74 us: local(): down = lax.ppermute(prev, 'sweep', [(i + 1, i) for i in range(n_sweep - 1)])]
    all_to_all x0 -> x1, waiting for transfers between devices: none -> 7.86 us  [local(): totals = lax.all_to_all(total, 'sweep', 0, 0, axis_index_groups=X_GROUPS)]
    all_to_all x0 -> x1, starting transfers between devices: none -> 6.65 us  [local(): totals = lax.all_to_all(total, 'sweep', 0, 0, axis_index_groups=X_GROUPS)]
    unnamed x10 -> x16, local copies, waits for them, and re-layouts: 0.02 us -> 4.59 us
  transfers between devices with their start and end apart: 5 -> 7, of which waited for: 2 -> 2; matrix products, arithmetic and copies ran while one was open for 2% -> 0% of each run, Pallas kernels for 0% -> 11%
where the time goes in v1:
time: 109 us
  blocking collectives  37.4 us (34%)
  starting transfers between devices  32.4 us (30%)
  Pallas kernels  23.2 us (21%)
  waiting for transfers between devices  8.84 us (8%)
  local copies, waits for them, and re-layouts  6.78 us (6%)
    all_to_all x1, blocking collectives, local(): recv = lax.all_to_all(send, 'sweep', 0, 0, axis_index_groups=Z_GROUPS)  23.5 us
    all_to_all x1, blocking collectives, local(): mine = lax.all_to_all(back, 'sweep', 0, 0, axis_index_groups=Z_GROUPS)  13.9 us
    ppermute x1, starting transfers between devices, local(): down = lax.ppermute(prev, 'sweep', [(i + 1, i) for i in range(n_sweep - 1)])  8.74 us
    all_to_all x1, waiting for transfers between devices, local(): totals = lax.all_to_all(total, 'sweep', 0, 0, axis_index_groups=X_GROUPS)  7.86 us
    all_to_all x1, starting transfers between devices, local(): totals = lax.all_to_all(total, 'sweep', 0, 0, axis_index_groups=X_GROUPS)  6.65 us
    ppermute x1, starting transfers between devices, local(): lax.ppermute(prev, 'span', [((i + 1) % n_span, i) for i in range(n_span)])  5.47 us
    ppermute x1, starting transfers between devices, local(): theirs = lax.ppermute(mine, 'sweep', swap)  5.29 us
    unnamed x16, local copies, waits for them, and re-layouts  4.59 us
  transfers between devices with their start and end apart: 7, of which 2 were waited for; matrix products, arithmetic and copies ran while one was open for 0% of the time, Pallas kernels for 11%

profile of v1, /device:TPU:1, one launch (start us, length us, event | category | flops | bytes accessed | tf_op | source)
XLA Modules:
  0.0 108.7 jit_solution(2355080130629112088)
XLA Ops:
  0.0 8.7 %collective-permute-start.1 = (bf16[6,135,128]{2,1,0:T(8,128)(2,1)}, bf16[6,135,128]{2,1,0:T(8,128)(2,1)S(1)}, u32[]{:S(2)}, u32[]{:S(2)}) collective-permute-start(bf16[6,135,128]{2,1,0:T(8,128)(2,1)} %bitcast.11), channel_id=1, source_target_pairs={{16,0},{32,16},{48,32},{64,48},{80,64},{96,80},{112,96},{128,112},... | collective-permute-start | bytes 622088 | tf_op jit(solution)/shard_map/ppermute | solution.py:228
  8.7 1.9 %collective-permute-start.2 = (bf16[6,135,128]{2,1,0:T(8,128)(2,1)}, bf16[6,135,128]{2,1,0:T(8,128)(2,1)S(1)}, u32[]{:S(2)}, u32[]{:S(2)}) collective-permute-start(bf16[6,135,128]{2,1,0:T(8,128)(2,1)} %bitcast.12), channel_id=1, source_target_pairs={{0,1},{1,2},{2,3},{3,4},{4,5},{5,6},{6,7},{7,8},{8,9},{9,10},{10,1... | collective-permute-start | bytes 622088 | tf_op jit(solution)/shard_map/ppermute | solution.py:226
  10.7 5.5 %collective-permute-start.3 = (bf16[6,135,128]{2,1,0:T(8,128)(2,1)}, bf16[6,135,128]{2,1,0:T(8,128)(2,1)S(1)}, u32[]{:S(2)}, u32[]{:S(2)}) collective-permute-start(bf16[6,135,128]{2,1,0:T(8,128)(2,1)} %bitcast.13), channel_id=1, source_target_pairs={{1,0},{2,1},{3,2},{4,3},{5,4},{6,5},{7,6},{8,7},{9,8},{10,9},{11,1... | collective-permute-start | bytes 622088 | tf_op jit(solution)/shard_map/ppermute | solution.py:227
  16.2 2.3 %transfer_kernel.1.own = f32[6,135,135]{2,1,0:T(8,128)} custom-call(bf16[6,135,135]{2,1,0:T(8,128)(2,1)} %bitcast.7, bf16[6,1,1,6,135,135]{5,4,3,2,1,0:T(8,128)(2,1)} %c3.1), custom_call_target="tpu_custom_call" | custom-call | tf_op jit(solution)/shard_map/transfer_kernel/pallas_call | solution.py:230
  18.5 1.9 %collective-permute-start = (f32[6,135,135]{2,1,0:T(8,128)}, f32[6,135,135]{2,1,0:T(8,128)S(1)}, u32[]{:S(2)}, u32[]{:S(2)}) collective-permute-start(f32[6,135,135]{2,1,0:T(8,128)} %transfer_kernel.1.own), channel_id=1, source_target_pairs={{0,16},{16,0},{32,48},{48,32},{64,80},{80,64},{96,112},{112,96},{1... | collective-permute-start | bytes 1312208 | tf_op jit(solution)/shard_map/ppermute | solution.py:231
  20.4 2.4 %wall_kernel.1.partial = f32[6,135,128]{2,1,0:T(8,128)} custom-call(s32[6]{0:T(128)} %bitcast.15, bf16[6,1,1,6,135,135]{5,4,3,2,1,0:T(8,128)(2,1)} %c3.1, bf16[6,1,1,6,135,135]{5,4,3,2,1,0:T(8,128)(2,1)} %c3.1, bf16[6,135,128]{2,1,0:T(8,128)(2,1)} %bitcast.10, bf16[6,135,128]{2,1,0:T(8,128)(2,1)} %bitcast.14), custom_call_target="tpu_custom_call" | custom-call | tf_op jit(solution)/shard_map/wall_kernel/pallas_call | solution.py:232
  22.8 0.0 collective-permute-done.1.down
  22.8 0.0 copy-start.4
  22.8 0.0 collective-permute-done.2.lower
  22.8 0.0 copy-start.5
  22.8 0.0 collective-permute-done.3.upper
  22.8 0.7 copy-done.4
  23.5 0.1 copy-done.5
  23.6 0.0 copy-start.6
  23.6 0.7 copy-done.6
  24.2 4.2 %offset_kernel.1.own = f32[6,135,128]{2,1,0:T(8,128)} custom-call(bf16[6,135,135]{2,1,0:T(8,128)(2,1)} %bitcast.8, bf16[6,1,1,6,135,135]{5,4,3,2,1,0:T(8,128)(2,1)} %c3.1, bf16[6,1,1,6,135,135]{5,4,3,2,1,0:T(8,128)(2,1)} %c3.1, bf16[6,1,1,6,135,135]{5,4,3,2,1,0:T(8,128)(2,1)} %c3.1, f32[6,135,128]{2,1,0:T(8,128)} %wall_kernel.1.partial, ...), custom_call_target="tpu_custom_call" | custom-call | tf_op jit(solution)/shard_map/offset_kernel/pallas_call | solution.py:239
  28.4 2.4 %collective-permute-start.4 = (f32[6,135,128]{2,1,0:T(8,128)}, f32[6,135,128]{2,1,0:T(8,128)S(1)}, u32[]{:S(2)}, u32[]{:S(2)}) collective-permute-start(f32[6,135,128]{2,1,0:T(8,128)} %offset_kernel.1.own), channel_id=1, source_target_pairs={{0,16},{16,0},{32,48},{48,32},{64,80},{80,64},{96,112},{112,96},{1... | collective-permute-start | bytes 1244168 | tf_op jit(solution)/shard_map/ppermute | solution.py:242
  30.8 0.0 collective-permute-done.sib
  30.9 0.0 copy-start.1
  30.9 0.9 copy-done.1
  31.8 3.3 %pair_kernel.1 = (bf16[3,3,136,128]{3,2,1,0:T(8,128)(2,1)}, bf16[6,2,135,135]{3,2,1,0:T(8,128)(2,1)}, bf16[6,2,135,135]{3,2,1,0:T(8,128)(2,1)}) custom-call(s32[1]{0:T(128)} %bitcast.core, f32[6,135,135]{2,1,0:T(8,128)} %transfer_kernel.1.own, f32[6,135,135]{2,1,0:T(8,128)} %copy-done.1), custom_call_target="tpu_custom_call" | custom-call | tf_op jit(solution)/shard_map/pair_kernel/pallas_call | solution.py:233
  35.1 0.0 collective-permute-done.4.sib
  35.1 0.0 copy-start.3
  35.1 0.7 copy-done.3
  35.8 3.1 %send_kernel.1 = (bf16[4,5,136,128]{3,2,1,0:T(8,128)(2,1)}, f32[6,135,128]{2,1,0:T(8,128)}) custom-call(s32[1]{0:T(128)} %bitcast.core, bf16[6,2,135,135]{3,2,1,0:T(8,128)(2,1)} %get-tuple-element.13.second, f32[6,135,128]{2,1,0:T(8,128)} %offset_kernel.1.own, f32[6,135,128]{2,1,0:T(8,128)} %copy-done.3, bf16[3,3,136,128]{3,2,1,0:T(8,128)(2,1)} %get-tuple-element.14.packed), custom_call_target="tpu_custom_call" | custom-call | tf_op jit(solution)/shard_map/send_kernel/pallas_call | solution.py:243
  38.9 23.5 %all_to_all.15.recv = bf16[4,5,136,128]{3,2,1,0:T(8,128)(2,1)} all-to-all(bf16[4,5,136,128]{3,2,1,0:T(8,128)(2,1)} %get-tuple-element.16), channel_id=1, replica_groups={{0,32,64,96},{16,48,80,112},{128,160,192,224},{144,176,208,240},{256,28..., dimensions={0} | all-to-all | bytes 1392640 | tf_op jit(solution)/shard_map/all_to_all | solution.py:246
  62.4 3.1 %chain_kernel.1 = (bf16[3,5,136,128]{3,2,1,0:T(8,128)(2,1)}, bf16[4,5,136,128]{3,2,1,0:T(8,128)(2,1)}) custom-call(bf16[4,5,136,128]{3,2,1,0:T(8,128)(2,1)} %all_to_all.15.recv), custom_call_target="tpu_custom_call" | custom-call | tf_op jit(solution)/shard_map/chain_kernel/pallas_call | solution.py:248
  65.5 6.7 %all-to-all-start.1 = ((bf16[4,5,136,128]{3,2,1,0:T(8,128)(2,1)}), bf16[4,5,136,128]{3,2,1,0:T(8,128)(2,1)S(1)}, u32[]{:S(2)}, u32[]{:S(2)}) async-start(bf16[4,5,136,128]{3,2,1,0:T(8,128)(2,1)} %get-tuple-element.17), calls=%async_computation.1 | async-start | bytes 1392640 | tf_op jit(solution)/shard_map/all_to_all | solution.py:254
  72.2 7.9 %all-to-all-done.1.totals = bf16[4,5,136,128]{3,2,1,0:T(8,128)(2,1)S(1)} async-done(((bf16[4,5,136,128]{3,2,1,0:T(8,128)(2,1)}), bf16[4,5,136,128]{3,2,1,0:T(8,128)(2,1)S(1)}, u32[]{:S(2)}, u32[]{:S(2)}) %all-to-all-start.1) | async-done | bytes 696352 | tf_op jit(solution)/shard_map/all_to_all | solution.py:254
  80.0 0.0 copy-start
  80.0 0.9 copy-done
  80.9 2.3 %state_kernel.1 = bf16[4,136,128]{2,1,0:T(8,128)(2,1)} custom-call(s32[1]{0:T(128)} %bitcast.5.place, bf16[4,5,136,128]{3,2,1,0:T(8,128)(2,1)} %copy-done, bf16[3,5,136,128]{3,2,1,0:T(8,128)(2,1)} %get-tuple-element.18.prefix), custom_call_target="tpu_custom_call" | custom-call | tf_op jit(solution)/shard_map/state_kernel/pallas_call | solution.py:255
  83.3 13.9 %all_to_all.16.own = bf16[4,136,128]{2,1,0:T(8,128)(2,1)S(1)} all-to-all(bf16[4,136,128]{2,1,0:T(8,128)(2,1)} %state_kernel.1), channel_id=1, replica_groups={{0,32,64,96},{16,48,80,112},{128,160,192,224},{144,176,208,240},{256,28..., dimensions={0} | all-to-all | bytes 278528 | tf_op jit(solution)/shard_map/all_to_all | solution.py:261
  97.1 0.0 copy-start.2
  97.1 5.3 %collective-permute-start.5 = (bf16[4,136,128]{2,1,0:T(8,128)(2,1)S(1)}, bf16[4,136,128]{2,1,0:T(8,128)(2,1)S(1)}, u32[]{:S(2)}, u32[]{:S(2)}) collective-permute-start(bf16[4,136,128]{2,1,0:T(8,128)(2,1)S(1)} %all_to_all.16.own), channel_id=1, source_target_pairs={{0,16},{16,0},{32,48},{48,32},{64,80},{80,64},{96,112},{112,96},{1... | collective-permute-start | bytes 417800 | tf_op jit(solution)/shard_map/ppermute | solution.py:262
  102.4 1.0 collective-permute-done.5.sib
  103.4 0.0 copy-start.7
  103.4 0.0 copy-done.2
  103.4 0.6 copy-done.7
  104.0 2.5 %final_kernel.1 = f32[6,135,128]{2,1,0:T(8,128)} custom-call(s32[1]{0:T(128)} %bitcast.core, bf16[6,2,135,135]{3,2,1,0:T(8,128)(2,1)} %get-tuple-element.12.matrix, f32[6,135,128]{2,1,0:T(8,128)} %get-tuple-element.15.shift, bf16[4,136,128]{2,1,0:T(8,128)(2,1)} %copy-done.2, bf16[4,136,128]{2,1,0:T(8,128)(2,1)} %copy-done.7), custom_call_target="tpu_custom_call" | custom-call | tf_op jit(solution)/shard_map/final_kernel/pallas_call | solution.py:263
  106.5 2.2 %copy.6 = f32[1,1,6,135,128]{4,1,3,2,0:T(1,128)} copy(f32[1,1,6,135,128]{4,3,2,1,0:T(8,128)} %bitcast.9) | data formatting | bytes 829440 | tf_op jit(solution)/shard_map/broadcast_in_dim | solution.py:264
Async XLA Ops:
  0.0 22.8 %collective-permute-start.1 = (bf16[6,135,128]{2,1,0:T(8,128)(2,1)}, bf16[6,135,128]{2,1,0:T(8,128)(2,1)S(1)}, u32[]{:S(2)}, u32[]{:S(2)}) collective-permute-start(bf16[6,135,128]{2,1,0:T(8,128)(2,1)} %bitcast.11), channel_id=1, source_target_pairs={{16,0},{32,16},{48,32},{64,48},{80,64},{96,80},{112,96},{128,112},... | collective-permute-start | bytes 622088 | tf_op jit(solution)/shard_map/ppermute | solution.py:228
  8.7 14.1 %collective-permute-start.2 = (bf16[6,135,128]{2,1,0:T(8,128)(2,1)}, bf16[6,135,128]{2,1,0:T(8,128)(2,1)S(1)}, u32[]{:S(2)}, u32[]{:S(2)}) collective-permute-start(bf16[6,135,128]{2,1,0:T(8,128)(2,1)} %bitcast.12), channel_id=1, source_target_pairs={{0,1},{1,2},{2,3},{3,4},{4,5},{5,6},{6,7},{7,8},{8,9},{9,10},{10,1... | collective-permute-start | bytes 622088 | tf_op jit(solution)/shard_map/ppermute | solution.py:226
  10.7 12.2 %collective-permute-start.3 = (bf16[6,135,128]{2,1,0:T(8,128)(2,1)}, bf16[6,135,128]{2,1,0:T(8,128)(2,1)S(1)}, u32[]{:S(2)}, u32[]{:S(2)}) collective-permute-start(bf16[6,135,128]{2,1,0:T(8,128)(2,1)} %bitcast.13), channel_id=1, source_target_pairs={{1,0},{2,1},{3,2},{4,3},{5,4},{6,5},{7,6},{8,7},{9,8},{10,9},{11,1... | collective-permute-start | bytes 622088 | tf_op jit(solution)/shard_map/ppermute | solution.py:227
  18.5 12.4 %collective-permute-start = (f32[6,135,135]{2,1,0:T(8,128)}, f32[6,135,135]{2,1,0:T(8,128)S(1)}, u32[]{:S(2)}, u32[]{:S(2)}) collective-permute-start(f32[6,135,135]{2,1,0:T(8,128)} %transfer_kernel.1.own), channel_id=1, source_target_pairs={{0,16},{16,0},{32,48},{48,32},{64,80},{80,64},{96,112},{112,96},{1... | collective-permute-start | bytes 1312208 | tf_op jit(solution)/shard_map/ppermute | solution.py:231
  22.8 0.7 copy-start.4
  22.8 0.7 copy-start.5
  23.6 0.7 copy-start.6
  28.4 6.7 %collective-permute-start.4 = (f32[6,135,128]{2,1,0:T(8,128)}, f32[6,135,128]{2,1,0:T(8,128)S(1)}, u32[]{:S(2)}, u32[]{:S(2)}) collective-permute-start(f32[6,135,128]{2,1,0:T(8,128)} %offset_kernel.1.own), channel_id=1, source_target_pairs={{0,16},{16,0},{32,48},{48,32},{64,80},{80,64},{96,112},{112,96},{1... | collective-permute-start | bytes 1244168 | tf_op jit(solution)/shard_map/ppermute | solution.py:242
  30.9 0.9 copy-start.1
  35.1 0.7 copy-start.3
  65.5 14.5 %all-to-all-start.1 = ((bf16[4,5,136,128]{3,2,1,0:T(8,128)(2,1)}), bf16[4,5,136,128]{3,2,1,0:T(8,128)(2,1)S(1)}, u32[]{:S(2)}, u32[]{:S(2)}) async-start(bf16[4,5,136,128]{3,2,1,0:T(8,128)(2,1)} %get-tuple-element.17), calls=%async_computation.1 | async-start | bytes 1392640 | tf_op jit(solution)/shard_map/all_to_all | solution.py:254
  80.0 0.9 copy-start
  97.1 6.3 %copy-start.2 = (bf16[4,136,128]{2,1,0:T(8,128)(2,1)}, bf16[4,136,128]{2,1,0:T(8,128)(2,1)S(1)}, u32[]{:S(2)}) copy-start(bf16[4,136,128]{2,1,0:T(8,128)(2,1)S(1)} %all_to_all.16.own) | copy-start | bytes 417796
  97.1 6.3 %collective-permute-start.5 = (bf16[4,136,128]{2,1,0:T(8,128)(2,1)S(1)}, bf16[4,136,128]{2,1,0:T(8,128)(2,1)S(1)}, u32[]{:S(2)}, u32[]{:S(2)}) collective-permute-start(bf16[4,136,128]{2,1,0:T(8,128)(2,1)S(1)} %all_to_all.16.own), channel_id=1, source_target_pairs={{0,16},{16,0},{32,48},{48,32},{64,80},{80,64},{96,112},{112,96},{1... | collective-permute-start | bytes 417800 | tf_op jit(solution)/shard_map/ppermute | solution.py:262
  103.4 0.7 copy-start.7

commit v2 on v1

v2 whole, which is shorter than its diff:
```python
import jax
import jax.numpy as jnp
from jax import lax
from jax.experimental import pallas as pl
from jax.experimental.pallas import tpu as pltpu
from jax.sharding import PartitionSpec as P


BS, NRHS, NZ = 135, 128, 6
LANE = 128
HALF = NZ // 2
RUN = 4
GROUPS = 4
ROWS = 136
SECOND, TAILS, FOLD = 144, 288, 24
PACKED = TAILS + FOLD
F32, BF16 = jnp.float32, jnp.bfloat16

RUNS = [[(g * RUN + m) * 2 + c for m in range(RUN)] for g in range(GROUPS) for c in range(2)]
ACROSS = [[(g * RUN + m) * 2 + c for g in range(GROUPS)] for m in range(RUN) for c in range(2)]
SHIFT = PACKED + 8
LOW = SHIFT + SECOND
AFFINE = LOW + SECOND


def mm(a, b):
    return jnp.dot(a, b, preferred_element_type=F32)


def split(v):
    hi = v.astype(BF16)
    return hi, (v - hi.astype(F32)).astype(BF16)


def mm3(a, b):
    return mm(a[0], b[0]) + (mm(a[0], b[1]) + mm(a[1], b[0]))


def pack(ref, at, pair, scratch):
    for k in range(2):
        ref[at + (slice(k * SECOND, k * SECOND + BS),)] = pair[k][:, :LANE].astype(BF16)
        scratch[k, :BS, :BS] = pair[k].astype(F32)
    both = scratch[0, :, LANE:] + pltpu.roll(scratch[1, :, LANE:], 8, 1)
    fold = both[:FOLD]
    for g in range(1, SECOND // FOLD):
        fold = fold + pltpu.roll(both[g * FOLD : (g + 1) * FOLD], 16 * g, 1)
    ref[at + (slice(TAILS, PACKED),)] = fold.astype(BF16)


def unpack(ref, at, scratch):
    fold = ref[at + (slice(TAILS, PACKED),)].astype(F32)
    lane = lax.broadcasted_iota(jnp.int32, fold.shape, 1)
    for g in range(SECOND // FOLD):
        rows = slice(g * FOLD, (g + 1) * FOLD)
        for k in range(2):
            shift = (2 * LANE - 16 * g - 8 * k) % LANE
            part = pltpu.roll(fold, shift, 1) if shift else fold
            scratch[k, rows, LANE:] = jnp.where(lane < 8, part, 0.0).astype(BF16)
    for k in range(2):
        scratch[k, :BS, :LANE] = ref[at + (slice(k * SECOND, k * SECOND + BS),)]
    return scratch[0, :BS, :BS], scratch[1, :BS, :BS]


def pack_shift(ref, at, value):
    ref[at + (slice(SHIFT, SHIFT + BS),)], ref[at + (slice(LOW, LOW + BS),)] = split(value)


def unpack_shift(ref, at):
    return ref[at + (slice(SHIFT, SHIFT + BS),)].astype(F32) + ref[at + (slice(LOW, LOW + BS),)].astype(F32)


def transfer_kernel(inv, c0, out):
    for s in range(NZ):
        out[s] = -mm(inv[s], c0[s])


def wall_kernel(layers, c, rhs, prev, out):
    for s in range(NZ):
        layer = layers[s]
        total = rhs[s].astype(F32)
        for step, index in ((-1, 0), (1, 1)):
            found, exists = 0, 0
            for t in range(NZ):
                match = layers[t] == layer + step
                found = jnp.where(match, t, found)
                exists = jnp.where(match, 1, exists)
            keep = jnp.full((BS, NRHS), exists, jnp.int32) > 0
            vectors = jnp.where(keep, prev[found].astype(F32), 0.0).astype(BF16)
            total = total - mm(c[index, s], vectors)
        out[s] = total


def offset_kernel(inv, c, partial, down, lower, upper, out):
    for s in range(NZ):
        total = mm(c[0, s], down[s]) + mm(c[1, s], lower[s]) + mm(c[2, s], upper[s])
        forcing = (partial[s] - total).astype(BF16)
        out[s] = mm(inv[s], forcing)


def pair_kernel(core, own, sib, packed, second_out, final_out, wide):
    c = core[0]
    wide[...] = jnp.zeros_like(wide)

    def body(first, second, mine):
        for s in range(NZ):
            t0, t1 = split(first[s]), split(second[s])
            second_out[s, 0], second_out[s, 1] = t1
            if mine == 0:
                final_out[s, 0], final_out[s, 1] = t0
                if s >= HALF:
                    continue
            both = split(mm3(t1, t0))
            if mine == 1:
                final_out[s, 0], final_out[s, 1] = both
            if s // HALF == mine:
                pack(packed, (s % HALF,), both, wide)

    pl.when(c == 0)(lambda: body(own, sib, 0))
    pl.when(c == 1)(lambda: body(sib, own, 1))


def send_kernel(core, second, own, sib, packed, send, shift_out):
    c = core[0]
    for s in range(HALF):
        send[s, :PACKED] = packed[s]
    send[HALF] = jnp.zeros_like(send[HALF])

    def body(first_o, second_o, mine):
        for s in range(NZ):
            if mine == 0:
                shift_out[s] = first_o[s]
                if s >= HALF:
                    continue
            b = mm3((second[s, 0], second[s, 1]), split(first_o[s])) + second_o[s]
            if mine == 1:
                shift_out[s] = b
            if s // HALF == mine:
                pack_shift(send, (s % HALF,), b)

    pl.when(c == 0)(lambda: body(own, sib, 0))
    pl.when(c == 1)(lambda: body(sib, own, 1))


def chain_kernel(recv, prefix, shifts, total, mat, wide):
    wide[...] = jnp.zeros_like(wide)
    product, state = None, None
    for k in range(RUN):
        a = unpack(recv, (k,), mat.at[k])
        b = unpack_shift(recv, (k,))
        if k == 0:
            product, state = a, b
        else:
            product, state = split(mm3(a, product)), mm3(a, split(state)) + b
        if k < RUN - 1:
            prefix[k, 0], prefix[k, 1] = product
            shifts[k] = state
    for g in range(GROUPS):
        pack(total, (g,), product, wide)
        pack_shift(total, (g,), state)


def state_kernel(place, totals, prefix, shifts, send, state, mat):
    x = place[0]
    first = jnp.full((BS, NRHS), x, jnp.int32) > 0
    state[...] = jnp.where(first, unpack_shift(totals, (0,)), 0.0)
    for g in range(1, GROUPS - 1):

        @pl.when(x > g)
        def _(g=g):
            state[...] = mm3(unpack(totals, (g,), mat), split(state[...])) + unpack_shift(totals, (g,))

    inflow = split(state[...])
    send[0, :BS] = inflow[0]
    for k in range(1, RUN):
        send[k, :BS] = (mm3((prefix[k - 1, 0], prefix[k - 1, 1]), inflow) + shifts[k - 1]).astype(BF16)


def final_kernel(core, matrix, shift, own, sib, out):
    c = core[0]

    def body(mine):
        for s in range(NZ):
            source = own if s // HALF == mine else sib
            v = source[s % HALF, :BS]
            out[s * BS : (s + 1) * BS] = shift[s] + (mm(matrix[s, 0], v) + mm(matrix[s, 1], v))

    pl.when(c == 0)(lambda: body(0))
    pl.when(c == 1)(lambda: body(1))


VMEM = pl.BlockSpec(memory_space=pltpu.VMEM)
SMEM = pl.BlockSpec(memory_space=pltpu.SMEM)
PARAMS = pltpu.CompilerParams(vmem_limit_bytes=20 << 20)


def hbm(*dims, dtype=F32):
    return jax.ShapeDtypeStruct(dims, dtype)


def vmem(*dims, dtype=F32):
    return pltpu.VMEM(dims, dtype)


def call(kernel, outs, args, scratch=()):
    scalar = [a.dtype == jnp.int32 for a in args]
    args = [a if one else pltpu.with_memory_space_constraint(a, pltpu.VMEM) for a, one in zip(args, scalar)]
    return pl.pallas_call(
        kernel,
        out_shape=outs,
        in_specs=[SMEM if one else VMEM for one in scalar],
        out_specs=jax.tree.map(lambda _: VMEM, outs, is_leaf=lambda o: not isinstance(o, tuple)),
        scratch_shapes=scratch,
        name=kernel.__name__,
        compiler_params=PARAMS,
    )(*args)


def local(inverses, couplings, rhs, previous, slot_layer):
    inv, rhs, prev, layers = inverses[0, 0], rhs[0, 0], previous[0, 0], slot_layer[0, 0]
    faces = couplings[:, 0, 0]
    place = lax.axis_index("sweep")
    core = (place % 2).reshape(1).astype(jnp.int32)
    group = (place // (2 * RUN)).reshape(1).astype(jnp.int32)
    n_sweep, n_span = lax.axis_size("sweep"), lax.axis_size("span")
    swap = [(i, i ^ 1) for i in range(n_sweep)]
    wide = pltpu.VMEM((2, SECOND, 2 * LANE), F32)

    lower = lax.ppermute(prev, "span", [(i, (i + 1) % n_span) for i in range(n_span)])
    upper = lax.ppermute(prev, "span", [((i + 1) % n_span, i) for i in range(n_span)])
    down = lax.ppermute(prev, "sweep", [(i + 1, i) for i in range(n_sweep - 1)])

    t_own = call(transfer_kernel, hbm(NZ, BS, BS), [inv, faces[0]])
    t_sib = lax.ppermute(t_own, "sweep", swap)
    partial = call(wall_kernel, vmem(NZ, BS, NRHS), [layers, faces[4:6], rhs, prev])
    packed, second, matrix = call(
        pair_kernel,
        (
            vmem(HALF, PACKED, LANE, dtype=BF16),
            vmem(NZ, 2, BS, BS, dtype=BF16),
            hbm(NZ, 2, BS, BS, dtype=BF16),
        ),
        [core, t_own, t_sib],
        [wide],
    )
    o_own = call(offset_kernel, hbm(NZ, BS, NRHS), [inv, faces[1:4], partial, down, lower, upper])
    o_sib = lax.ppermute(o_own, "sweep", swap)
    send, shift = call(
        send_kernel,
        (hbm(RUN, AFFINE, LANE, dtype=BF16), hbm(NZ, BS, NRHS)),
        [core, second, o_own, o_sib, packed],
    )
    maps = lax.all_to_all(send, "sweep", 0, 0, axis_index_groups=RUNS)
    prefix, shifts, total = call(
        chain_kernel,
        (
            vmem(RUN - 1, 2, BS, BS, dtype=BF16),
            vmem(RUN - 1, BS, NRHS),
            hbm(GROUPS, AFFINE, LANE, dtype=BF16),
        ),
        [maps],
        [pltpu.VMEM((RUN, 2, SECOND, 2 * LANE), BF16), wide],
    )
    totals = lax.all_to_all(total, "sweep", 0, 0, axis_index_groups=ACROSS)
    back = call(
        state_kernel,
        hbm(RUN, ROWS, NRHS, dtype=BF16),
        [group, totals, prefix, shifts],
        [pltpu.VMEM((BS, NRHS), F32), pltpu.VMEM((2, SECOND, 2 * LANE), BF16)],
    )
    mine = lax.all_to_all(back, "sweep", 0, 0, axis_index_groups=RUNS)
    theirs = lax.ppermute(mine, "sweep", swap)
    out = call(final_kernel, hbm(NZ * BS, NRHS), [core, matrix, shift, mine, theirs])
    return out.reshape(1, 1, NZ, BS, NRHS)


def solution(mesh):
    return jax.shard_map(
        local,
        mesh=mesh,
        in_specs=(
            P("sweep", "span", None, None, None),
            P(None, "sweep", "span", None, None, None),
            P("sweep", "span", None, None, None),
            P("sweep", "span", None, None, None),
            P("sweep", "span", None),
        ),
        out_specs=P("sweep", "span", None, None, None),
        check_vma=False,
    )
```

time: 109 us -> 89.2 us (0.82)
  Pallas kernels: 23.2 us -> 6.89 us
  starting transfers between devices: 32.4 us -> 29.2 us
    pallas_call x8, Pallas kernels: 23.2 us -> 6.89 us  [call(): pl.pallas_call(kernel, out_shape=outs, in_specs=[SMEM if one else VMEM fo...]
    ppermute x1, starting transfers between devices: 8.74 us -> 4.95 us  [local(): down = lax.ppermute(prev, 'sweep', [(i + 1, i) for i in range(n_sweep - 1)])]
    unnamed x16 -> x10, local copies, waits for them, and re-layouts: 4.59 us -> 1.02 us
    all_to_all x1, starting transfers between devices: 6.65 us -> 3.48 us  [local(): totals = lax.all_to_all(total, 'sweep', 0, 0, axis_index_groups=ACROSS)]
    slice x0 -> x2, local copies, waits for them, and re-layouts: none -> 2.64 us  [the longest x1 1.43 us: local(): faces[1:4]]
    ppermute x1, starting transfers between devices: 5.47 us -> 7.71 us  [local(): lax.ppermute(prev, 'span', [((i + 1) % n_span, i) for i in range(n_span)])]
    broadcast_in_dim x1 -> x0, local copies, waits for them, and re-layouts: 2.18 us -> none  [local(): return out[None, None]]
    ppermute x1, starting transfers between devices: 5.29 us -> 6.68 us  [local(): theirs = lax.ppermute(mine, 'sweep', swap)]
  transfers between devices with their start and end apart: 7 -> 7, of which waited for: 2 -> 3; matrix products, arithmetic and copies ran while one was open for 0% -> 4% of each run, Pallas kernels for 11% -> 4%
where the time goes in v2:
time: 89.2 us; the launch traced here: 88.3 us
  blocking collectives  37.2 us (42%)
  starting transfers between devices  29.2 us (33%)
  waiting for transfers between devices  8.98 us (10%)
  Pallas kernels  6.89 us (8%)
  local copies, waits for them, and re-layouts  5.86 us (7%)
    all_to_all x1, blocking collectives, local(): maps = lax.all_to_all(send, 'sweep', 0, 0, axis_index_groups=RUNS)  24.6 us
    all_to_all x1, blocking collectives, local(): mine = lax.all_to_all(back, 'sweep', 0, 0, axis_index_groups=RUNS)  12.6 us
    ppermute x1, starting transfers between devices, local(): lax.ppermute(prev, 'span', [((i + 1) % n_span, i) for i in range(n_span)])  7.71 us
    all_to_all x1, waiting for transfers between devices, local(): totals = lax.all_to_all(total, 'sweep', 0, 0, axis_index_groups=ACROSS)  7.41 us
    pallas_call x8, Pallas kernels, call(): pl.pallas_call(kernel, out_shape=outs, in_specs=[SMEM if one else VMEM fo...  6.89 us
    ppermute x1, starting transfers between devices, local(): theirs = lax.ppermute(mine, 'sweep', swap)  6.68 us
    ppermute x1, starting transfers between devices, local(): down = lax.ppermute(prev, 'sweep', [(i + 1, i) for i in range(n_sweep - 1)])  4.95 us
    all_to_all x1, starting transfers between devices, local(): totals = lax.all_to_all(total, 'sweep', 0, 0, axis_index_groups=ACROSS)  3.48 us
  transfers between devices with their start and end apart: 7, of which 3 were waited for; matrix products, arithmetic and copies ran while one was open for 4% of the time, Pallas kernels for 4%

profile of v2, /device:TPU:1, one launch (start us, length us, event | category | flops | bytes accessed | tf_op | source)
XLA Modules:
  0.0 88.3 jit_solution(2602938372321891856)
XLA Ops:
  0.0 7.7 %collective-permute-start.3 = (bf16[6,135,128]{2,1,0:T(8,128)(2,1)}, bf16[6,135,128]{2,1,0:T(8,128)(2,1)S(1)}, u32[]{:S(2)}, u32[]{:S(2)}) collective-permute-start(bf16[6,135,128]{2,1,0:T(8,128)(2,1)} %bitcast.16), channel_id=1, source_target_pairs={{1,0},{2,1},{3,2},{4,3},{5,4},{6,5},{7,6},{8,7},{9,8},{10,9},{11,1... | collective-permute-start | bytes 622088 | tf_op jit(solution)/shard_map/ppermute | solution.py:229
  7.7 1.9 %collective-permute-start.2 = (bf16[6,135,128]{2,1,0:T(8,128)(2,1)}, bf16[6,135,128]{2,1,0:T(8,128)(2,1)S(1)}, u32[]{:S(2)}, u32[]{:S(2)}) collective-permute-start(bf16[6,135,128]{2,1,0:T(8,128)(2,1)} %bitcast.17), channel_id=1, source_target_pairs={{0,1},{1,2},{2,3},{3,4},{4,5},{5,6},{6,7},{7,8},{8,9},{9,10},{10,1... | collective-permute-start | bytes 622088 | tf_op jit(solution)/shard_map/ppermute | solution.py:228
  9.7 4.9 %collective-permute-start.1 = (bf16[6,135,128]{2,1,0:T(8,128)(2,1)}, bf16[6,135,128]{2,1,0:T(8,128)(2,1)S(1)}, u32[]{:S(2)}, u32[]{:S(2)}) collective-permute-start(bf16[6,135,128]{2,1,0:T(8,128)(2,1)} %bitcast.18), channel_id=1, source_target_pairs={{16,0},{32,16},{48,32},{64,48},{80,64},{96,80},{112,96},{128,112},... | collective-permute-start | bytes 622088 | tf_op jit(solution)/shard_map/ppermute | solution.py:230
  14.6 1.0 %slice_bitcast_fusion.2.c0 = bf16[6,135,135]{2,1,0:T(8,128)(2,1)S(1)} fusion(bf16[6,1,1,6,135,135]{5,4,3,2,1,0:T(8,128)(2,1)} %param.6), kind=kLoop, calls=%fused_computation.2 | loop fusion | bytes 437400 | tf_op jit(solution)/shard_map/squeeze | solution.py:232
  15.6 0.0 copy-start
  15.7 1.0 %copy-done = bf16[1,1,6,135,135]{4,3,2,1,0:T(8,128)(2,1)S(1)} copy-done((bf16[1,1,6,135,135]{4,3,2,1,0:T(8,128)(2,1)S(1)}, bf16[1,1,6,135,135]{4,3,2,1,0:T(8,128)(2,1)}, u32[]{:S(2)}) %copy-start) | copy-done | bytes 218724
  16.7 0.3 transfer_kernel.1.own
  16.9 0.0 copy-start.2
  16.9 0.0 copy-start.3
  17.0 0.0 copy-start.4
  17.0 2.1 %collective-permute-start = (f32[6,135,135]{2,1,0:T(8,128)S(1)}, f32[6,135,135]{2,1,0:T(8,128)S(1)}, u32[]{:S(2)}, u32[]{:S(2)}) collective-permute-start(f32[6,135,135]{2,1,0:T(8,128)S(1)} %transfer_kernel.1.own), channel_id=1, source_target_pairs={{0,16},{16,0},{32,48},{48,32},{64,80},{80,64},{96,112},{112,96},{1... | collective-permute-start | bytes 1312208 | tf_op jit(solution)/shard_map/ppermute | solution.py:233
  19.0 0.0 copy-start.1
  19.0 1.4 %slice_bitcast_fusion.c = bf16[3,6,135,135]{3,2,1,0:T(8,128)(2,1)S(1)} fusion(bf16[6,1,1,6,135,135]{5,4,3,0,2,1:T(8,128)(2,1)} %bitcast.21), kind=kLoop, calls=%fused_computation | loop fusion | bytes 1312200 | tf_op jit(solution)/shard_map/slice | solution.py:245
  20.5 1.2 %slice_bitcast_fusion.1.c = bf16[2,6,135,135]{3,2,1,0:T(8,128)(2,1)S(1)} fusion(bf16[6,1,1,6,135,135]{5,4,3,0,2,1:T(8,128)(2,1)} %bitcast.22), kind=kLoop, calls=%fused_computation.1 | loop fusion | bytes 874800 | tf_op jit(solution)/shard_map/slice | solution.py:234
  21.7 0.0 copy-done.2
  21.7 0.0 copy-done.3
  21.7 0.0 copy-done.4
  21.7 0.9 %wall_kernel.1.partial = f32[6,135,128]{2,1,0:T(8,128)S(1)} custom-call(s32[6]{0:T(128)S(1)} %bitcast.20, bf16[2,6,135,135]{3,2,1,0:T(8,128)(2,1)S(1)} %slice_bitcast_fusion.1.c, bf16[6,135,128]{2,1,0:T(8,128)(2,1)S(1)} %bitcast.15, bf16[6,135,128]{2,1,0:T(8,128)(2,1)S(1)} %bitcast.19), custom_call_target="tpu_custom_call" | custom-call | tf_op jit(solution)/shard_map/wall_kernel/pallas_call | solution.py:207
  22.7 0.0 collective-permute-done.3.upper
  22.7 0.0 collective-permute-done.2.lower
  22.7 0.0 collective-permute-done.1.down
  22.7 0.0 copy-done.1
  22.7 1.7 %offset_kernel.1.own = f32[6,135,128]{2,1,0:T(8,128)S(1)} custom-call(bf16[6,135,135]{2,1,0:T(8,128)(2,1)S(1)} %bitcast.14, bf16[3,6,135,135]{3,2,1,0:T(8,128)(2,1)S(1)} %slice_bitcast_fusion.c, f32[6,135,128]{2,1,0:T(8,128)S(1)} %wall_kernel.1.partial, bf16[6,135,128]{2,1,0:T(8,128)(2,1)S(1)} %collective-permute-done.1.down, ...), custom_call_target="tpu_custom_call" | custom-call | tf_op jit(solution)/shard_map/offset_kernel/pallas_call | solution.py:207
  24.4 2.4 %collective-permute-start.4 = (f32[6,135,128]{2,1,0:T(8,128)S(1)}, f32[6,135,128]{2,1,0:T(8,128)S(1)}, u32[]{:S(2)}, u32[]{:S(2)}) collective-permute-start(f32[6,135,128]{2,1,0:T(8,128)S(1)} %offset_kernel.1.own), channel_id=1, source_target_pairs={{0,16},{16,0},{32,48},{48,32},{64,80},{80,64},{96,112},{112,96},{1... | collective-permute-start | bytes 1244168 | tf_op jit(solution)/shard_map/ppermute | solution.py:246
  26.9 0.0 collective-permute-done.sib
  26.9 0.8 pair_kernel.1
  27.6 0.6 collective-permute-done.4.sib
  28.2 0.5 send_kernel.1
  28.8 24.6 %all_to_all.15.recv = bf16[4,608,128]{2,1,0:T(8,128)(2,1)S(1)} all-to-all(bf16[4,608,128]{2,1,0:T(8,128)(2,1)S(1)} %get-tuple-element.17), channel_id=1, replica_groups={{0,32,64,96},{16,48,80,112},{128,160,192,224},{144,176,208,240},{256,28..., dimensions={0} | all-to-all | bytes 1245184 | tf_op jit(solution)/shard_map/all_to_all | solution.py:252
  53.4 1.9 %chain_kernel.1 = (bf16[3,2,135,135]{3,2,1,0:T(8,128)(2,1)S(1)}, f32[3,135,128]{2,1,0:T(8,128)S(1)}, bf16[4,608,128]{2,1,0:T(8,128)(2,1)}) custom-call(bf16[4,608,128]{2,1,0:T(8,128)(2,1)S(1)} %all_to_all.15.recv), custom_call_target="tpu_custom_call" | custom-call | tf_op jit(solution)/shard_map/chain_kernel/pallas_call | solution.py:207
  55.3 3.5 %all-to-all-start.1 = ((bf16[4,608,128]{2,1,0:T(8,128)(2,1)}), bf16[4,608,128]{2,1,0:T(8,128)(2,1)S(1)}, u32[]{:S(2)}, u32[]{:S(2)}) async-start(bf16[4,608,128]{2,1,0:T(8,128)(2,1)} %get-tuple-element.18), calls=%async_computation.1 | async-start | bytes 1245184 | tf_op jit(solution)/shard_map/all_to_all | solution.py:263
  58.8 7.4 %all-to-all-done.1.totals = bf16[4,608,128]{2,1,0:T(8,128)(2,1)S(1)} async-done(((bf16[4,608,128]{2,1,0:T(8,128)(2,1)}), bf16[4,608,128]{2,1,0:T(8,128)(2,1)S(1)}, u32[]{:S(2)}, u32[]{:S(2)}) %all-to-all-start.1) | async-done | bytes 622624 | tf_op jit(solution)/shard_map/all_to_all | solution.py:263
  66.2 0.3 state_kernel.1
  66.6 12.6 %all_to_all.16.own = bf16[4,136,128]{2,1,0:T(8,128)(2,1)S(1)} all-to-all(bf16[4,136,128]{2,1,0:T(8,128)(2,1)S(1)} %state_kernel.1), channel_id=1, replica_groups={{0,32,64,96},{16,48,80,112},{128,160,192,224},{144,176,208,240},{256,28..., dimensions={0} | all-to-all | bytes 278528 | tf_op jit(solution)/shard_map/all_to_all | solution.py:270
  79.1 6.7 %collective-permute-start.5 = (bf16[4,136,128]{2,1,0:T(8,128)(2,1)S(1)}, bf16[4,136,128]{2,1,0:T(8,128)(2,1)S(1)}, u32[]{:S(2)}, u32[]{:S(2)}) collective-permute-start(bf16[4,136,128]{2,1,0:T(8,128)(2,1)S(1)} %all_to_all.16.own), channel_id=1, source_target_pairs={{0,16},{16,0},{32,48},{48,32},{64,80},{80,64},{96,112},{112,96},{1... | collective-permute-start | bytes 417800 | tf_op jit(solution)/shard_map/ppermute | solution.py:271
  85.8 1.0 %collective-permute-done.5.sib = bf16[4,136,128]{2,1,0:T(8,128)(2,1)S(1)} collective-permute-done((bf16[4,136,128]{2,1,0:T(8,128)(2,1)S(1)}, bf16[4,136,128]{2,1,0:T(8,128)(2,1)S(1)}, u32[]{:S(2)}, u32[]{:S(2)}) %collective-permute-start.5) | collective-permute-done | bytes 139296 | tf_op jit(solution)/shard_map/ppermute | solution.py:271
  86.8 0.4 final_kernel.1
  87.2 1.2 %reshape.16 = f32[1,1,6,135,128]{4,1,3,2,0:T(1,128)} reshape(f32[810,128]{1,0:T(8,128)S(1)} %final_kernel.1) | data formatting | bytes 829440 | tf_op jit(solution)/shard_map/reshape | solution.py:273
Async XLA Ops:
  0.0 22.7 %collective-permute-start.3 = (bf16[6,135,128]{2,1,0:T(8,128)(2,1)}, bf16[6,135,128]{2,1,0:T(8,128)(2,1)S(1)}, u32[]{:S(2)}, u32[]{:S(2)}) collective-permute-start(bf16[6,135,128]{2,1,0:T(8,128)(2,1)} %bitcast.16), channel_id=1, source_target_pairs={{1,0},{2,1},{3,2},{4,3},{5,4},{6,5},{7,6},{8,7},{9,8},{10,9},{11,1... | collective-permute-start | bytes 622088 | tf_op jit(solution)/shard_map/ppermute | solution.py:229
  7.7 15.0 %collective-permute-start.2 = (bf16[6,135,128]{2,1,0:T(8,128)(2,1)}, bf16[6,135,128]{2,1,0:T(8,128)(2,1)S(1)}, u32[]{:S(2)}, u32[]{:S(2)}) collective-permute-start(bf16[6,135,128]{2,1,0:T(8,128)(2,1)} %bitcast.17), channel_id=1, source_target_pairs={{0,1},{1,2},{2,3},{3,4},{4,5},{5,6},{6,7},{7,8},{8,9},{9,10},{10,1... | collective-permute-start | bytes 622088 | tf_op jit(solution)/shard_map/ppermute | solution.py:228
  9.7 13.0 %collective-permute-start.1 = (bf16[6,135,128]{2,1,0:T(8,128)(2,1)}, bf16[6,135,128]{2,1,0:T(8,128)(2,1)S(1)}, u32[]{:S(2)}, u32[]{:S(2)}) collective-permute-start(bf16[6,135,128]{2,1,0:T(8,128)(2,1)} %bitcast.18), channel_id=1, source_target_pairs={{16,0},{32,16},{48,32},{64,48},{80,64},{96,80},{112,96},{128,112},... | collective-permute-start | bytes 622088 | tf_op jit(solution)/shard_map/ppermute | solution.py:230
  15.6 1.0 %copy-start = (bf16[1,1,6,135,135]{4,3,2,1,0:T(8,128)(2,1)S(1)}, bf16[1,1,6,135,135]{4,3,2,1,0:T(8,128)(2,1)}, u32[]{:S(2)}) copy-start(bf16[1,1,6,135,135]{4,3,2,1,0:T(8,128)(2,1)} %param.5) | copy-start | bytes 656104
  16.9 4.8 %copy-start.2 = (bf16[1,1,6,135,128]{4,3,2,1,0:T(8,128)(2,1)S(1)}, bf16[1,1,6,135,128]{4,3,2,1,0:T(8,128)(2,1)}, u32[]{:S(2)}) copy-start(bf16[1,1,6,135,128]{4,3,2,1,0:T(8,128)(2,1)} %param.7) | copy-start | bytes 622084
  16.9 4.8 %copy-start.3 = (bf16[1,1,6,135,128]{4,3,2,1,0:T(8,128)(2,1)S(1)}, bf16[1,1,6,135,128]{4,3,2,1,0:T(8,128)(2,1)}, u32[]{:S(2)}) copy-start(bf16[1,1,6,135,128]{4,3,2,1,0:T(8,128)(2,1)} %param.8) | copy-start | bytes 622084
  17.0 4.8 %copy-start.4 = (s32[1,1,6]{2,1,0:T(1,128)S(1)}, s32[1,1,6]{2,1,0:T(1,128)}, u32[]{:S(2)}) copy-start(s32[1,1,6]{2,1,0:T(1,128)} %param.9) | copy-start | bytes 76
  17.0 9.9 %collective-permute-start = (f32[6,135,135]{2,1,0:T(8,128)S(1)}, f32[6,135,135]{2,1,0:T(8,128)S(1)}, u32[]{:S(2)}, u32[]{:S(2)}) collective-permute-start(f32[6,135,135]{2,1,0:T(8,128)S(1)} %transfer_kernel.1.own), channel_id=1, source_target_pairs={{0,16},{16,0},{32,48},{48,32},{64,80},{80,64},{96,112},{112,96},{1... | collective-permute-start | bytes 1312208 | tf_op jit(solution)/shard_map/ppermute | solution.py:233
  19.0 3.7 %copy-start.1 = (bf16[1,1,6,135,135]{4,3,2,1,0:T(8,128)(2,1)S(1)}, bf16[1,1,6,135,135]{4,3,2,1,0:T(8,128)(2,1)}, u32[]{:S(2)}) copy-start(bf16[1,1,6,135,135]{4,3,2,1,0:T(8,128)(2,1)} %param.5) | copy-start | bytes 656104
  24.4 3.8 %collective-permute-start.4 = (f32[6,135,128]{2,1,0:T(8,128)S(1)}, f32[6,135,128]{2,1,0:T(8,128)S(1)}, u32[]{:S(2)}, u32[]{:S(2)}) collective-permute-start(f32[6,135,128]{2,1,0:T(8,128)S(1)} %offset_kernel.1.own), channel_id=1, source_target_pairs={{0,16},{16,0},{32,48},{48,32},{64,80},{80,64},{96,112},{112,96},{1... | collective-permute-start | bytes 1244168 | tf_op jit(solution)/shard_map/ppermute | solution.py:246
  55.3 10.9 %all-to-all-start.1 = ((bf16[4,608,128]{2,1,0:T(8,128)(2,1)}), bf16[4,608,128]{2,1,0:T(8,128)(2,1)S(1)}, u32[]{:S(2)}, u32[]{:S(2)}) async-start(bf16[4,608,128]{2,1,0:T(8,128)(2,1)} %get-tuple-element.18), calls=%async_computation.1 | async-start | bytes 1245184 | tf_op jit(solution)/shard_map/all_to_all | solution.py:263
  79.1 7.7 %collective-permute-start.5 = (bf16[4,136,128]{2,1,0:T(8,128)(2,1)S(1)}, bf16[4,136,128]{2,1,0:T(8,128)(2,1)S(1)}, u32[]{:S(2)}, u32[]{:S(2)}) collective-permute-start(bf16[4,136,128]{2,1,0:T(8,128)(2,1)S(1)} %all_to_all.16.own), channel_id=1, source_target_pairs={{0,16},{16,0},{32,48},{48,32},{64,80},{80,64},{96,112},{112,96},{1... | collective-permute-start | bytes 417800 | tf_op jit(solution)/shard_map/ppermute | solution.py:271

commit v3 on v2

v3 whole, which is shorter than its diff:
```python
import jax
import jax.numpy as jnp
from jax import lax
from jax.experimental import pallas as pl
from jax.experimental.pallas import tpu as pltpu
from jax.sharding import PartitionSpec as P


BS, NRHS, NZ = 135, 128, 6
LANE = 128
HALF = NZ // 2
RUN = 4
GROUPS = 4
ROWS = 136
SECOND, TAILS, FOLD = 144, 288, 24
PACKED = TAILS + FOLD
F32, BF16 = jnp.float32, jnp.bfloat16

RUNS = [[(g * RUN + m) * 2 + c for m in range(RUN)] for g in range(GROUPS) for c in range(2)]
ACROSS = [[(g * RUN + m) * 2 + c for g in range(GROUPS)] for m in range(RUN) for c in range(2)]
SHIFT = PACKED + 8
LOW = SHIFT + SECOND
CHIP = SHIFT + ROWS
AFFINE = LOW + ROWS


def mm(a, b):
    return jnp.dot(a, b, preferred_element_type=F32)


def split(v):
    hi = v.astype(BF16)
    return hi, (v - hi.astype(F32)).astype(BF16)


def mm3(a, b):
    return mm(a[0], b[0]) + (mm(a[0], b[1]) + mm(a[1], b[0]))


def pack(ref, at, pair, scratch):
    for k in range(2):
        ref[at + (slice(k * SECOND, k * SECOND + BS),)] = pair[k][:, :LANE].astype(BF16)
        scratch[k, :BS, :BS] = pair[k].astype(F32)
    both = scratch[0, :, LANE:] + pltpu.roll(scratch[1, :, LANE:], 8, 1)
    fold = both[:FOLD]
    for g in range(1, SECOND // FOLD):
        fold = fold + pltpu.roll(both[g * FOLD : (g + 1) * FOLD], 16 * g, 1)
    ref[at + (slice(TAILS, PACKED),)] = fold.astype(BF16)


def unpack(ref, at, scratch):
    fold = ref[at + (slice(TAILS, PACKED),)].astype(F32)
    lane = lax.broadcasted_iota(jnp.int32, fold.shape, 1)
    for g in range(SECOND // FOLD):
        rows = slice(g * FOLD, (g + 1) * FOLD)
        for k in range(2):
            shift = (2 * LANE - 16 * g - 8 * k) % LANE
            part = pltpu.roll(fold, shift, 1) if shift else fold
            scratch[k, rows, LANE:] = jnp.where(lane < 8, part, 0.0).astype(BF16)
    for k in range(2):
        scratch[k, :BS, :LANE] = ref[at + (slice(k * SECOND, k * SECOND + BS),)]
    return scratch[0, :BS, :BS], scratch[1, :BS, :BS]


def pack_shift(ref, at, value):
    ref[at + (slice(SHIFT, SHIFT + BS),)], ref[at + (slice(LOW, LOW + BS),)] = split(value)


def unpack_shift(ref, at):
    return ref[at + (slice(SHIFT, SHIFT + BS),)].astype(F32) + ref[at + (slice(LOW, LOW + BS),)].astype(F32)


def local_kernel(core, layers_in, inv_in, c_in, rhs_in, prev_in, inv, c1, transfer, send, partial, layers, c0, walls, rhs, prev, sems):
    moves = (
        (inv_in, inv),
        (c_in.at[0, 0, 0], c0),
        (prev_in, prev),
        (rhs_in, rhs),
        (layers_in, layers),
        (c_in.at[4, 0, 0], walls.at[0]),
        (c_in.at[5, 0, 0], walls.at[1]),
        (c_in.at[1, 0, 0], c1),
    )
    copies = [pltpu.make_async_copy(source, target, sems.at[i]) for i, (source, target) in enumerate(moves)]
    for copy in copies:
        copy.start()
    for copy in copies[:2]:
        copy.wait()
    for s in range(NZ):
        transfer[s, :BS, :BS] = -mm(inv[s], c0[s])
    other = HALF * (1 - core[0])
    for j in range(HALF):
        send[j] = transfer[other + j]
    for copy in copies[2:7]:
        copy.wait()
    for s in range(NZ):
        layer = layers[0, 0, s]
        total = rhs[s].astype(F32)
        for step, index in ((-1, 0), (1, 1)):
            found, exists = 0, 0
            for t in range(NZ):
                match = layers[0, 0, t] == layer + step
                found = jnp.where(match, t, found)
                exists = jnp.where(match, 1, exists)
            keep = jnp.full((BS, NRHS), exists, jnp.int32) > 0
            vectors = jnp.where(keep, prev[found].astype(F32), 0.0).astype(BF16)
            total = total - mm(walls[index, s], vectors)
        partial[s] = total
    for copy in copies[7:]:
        copy.wait()


def product_kernel(core, transfer, sib, packed, wide):
    c = core[0]
    wide[...] = jnp.zeros_like(wide)

    def body(mine):
        for j in range(HALF):
            own, got = split(transfer[mine * HALF + j, :BS, :BS]), split(sib[j, :BS, :BS])
            pack(packed, (j,), split(mm3(got, own) if mine == 0 else mm3(own, got)), wide)

    pl.when(c == 0)(lambda: body(0))
    pl.when(c == 1)(lambda: body(1))


def span_kernel(c_in, partial, lower, upper, out, c, sems):
    copies = [pltpu.make_async_copy(c_in.at[2 + i, 0, 0], c.at[i], sems.at[i]) for i in range(2)]
    for copy in copies:
        copy.start()
    for copy in copies:
        copy.wait()
    for s in range(NZ):
        out[s] = partial[s] - (mm(c[0, s], lower[s]) + mm(c[1, s], upper[s]))


def offset_kernel(core, inv, c1, partial, down, out, send):
    for s in range(NZ):
        forcing = (partial[s] - mm(c1[s], down[s])).astype(BF16)
        out[s] = mm(inv[s], forcing)
    other = HALF * (1 - core[0])
    for j in range(HALF):
        send[j, :BS] = out[other + j]


def pair_kernel(core, packed, transfer, sib, offset, offset_sib, send):
    c = core[0]
    send[HALF] = jnp.zeros_like(send[HALF])
    for j in range(HALF):
        send[j, :PACKED] = packed[j]

    def body(mine):
        for j in range(HALF):
            s = mine * HALF + j
            own, got = offset[s], offset_sib[j, :BS]
            first, second, t1 = (own, got, sib[j, :BS, :BS]) if mine == 0 else (got, own, transfer[s, :BS, :BS])
            send[j, SHIFT : SHIFT + BS] = (mm3(split(t1), split(first)) + second).astype(BF16)

    pl.when(c == 0)(lambda: body(0))
    pl.when(c == 1)(lambda: body(1))


def chain_kernel(recv, prefix, shifts, total, mat, wide):
    wide[...] = jnp.zeros_like(wide)
    product, state = None, None
    for k in range(RUN):
        a = unpack(recv, (k,), mat.at[k])
        b = recv[k, SHIFT : SHIFT + BS].astype(F32)
        if k == 0:
            product, state = a, b
        else:
            product, state = split(mm3(a, product)), mm3(a, split(state)) + b
        if k < RUN - 1:
            prefix[k, 0], prefix[k, 1] = product
            shifts[k] = state
    pack(total, (), product, wide)
    pack_shift(total, (), state)


def state_kernel(place, totals, prefix, shifts, send, state, mat):
    x = place[0]
    first = jnp.full((BS, NRHS), x, jnp.int32) > 0
    state[...] = jnp.where(first, unpack_shift(totals, (0,)), 0.0)
    for g in range(1, GROUPS - 1):

        @pl.when(x > g)
        def _(g=g):
            state[...] = mm3(unpack(totals, (g,), mat), split(state[...])) + unpack_shift(totals, (g,))

    inflow = split(state[...])
    send[0, :BS] = inflow[0]
    for k in range(1, RUN):
        send[k, :BS] = (mm3((prefix[k - 1, 0], prefix[k - 1, 1]), inflow) + shifts[k - 1]).astype(BF16)


def half_kernel(core, transfer, offset, sib, offset_sib, inflow, out, send):
    c = core[0]

    def body(mine):
        for j in range(HALF):
            s = mine * HALF + j
            t, o = split(transfer[s, :BS, :BS]), offset[s]
            v = inflow[j, :BS]
            if mine == 0:
                out[j] = o + (mm(t[0], v) + mm(t[1], v))
                send[j, :BS] = out[j].astype(BF16)
            else:
                first = split(sib[j, :BS, :BS])
                middle = offset_sib[j, :BS] + (mm(first[0], v) + mm(first[1], v))
                out[j] = o + mm3(t, split(middle))
                send[j, :BS] = v

    pl.when(c == 0)(lambda: body(0))
    pl.when(c == 1)(lambda: body(1))


def final_kernel(core, transfer, offset, half, inflow, out):
    c = core[0]

    def body(mine):
        for j in range(HALF):
            s = mine * HALF + j
            out[s * BS : (s + 1) * BS, 0] = half[j]
        for j in range(HALF):
            s = (1 - mine) * HALF + j
            t, v = split(transfer[s, :BS, :BS]), inflow[j, :BS]
            out[s * BS : (s + 1) * BS, 0] = offset[s] + (mm(t[0], v) + mm(t[1], v))

    pl.when(c == 0)(lambda: body(0))
    pl.when(c == 1)(lambda: body(1))


VMEM = pl.BlockSpec(memory_space=pltpu.VMEM)
SMEM = pl.BlockSpec(memory_space=pltpu.SMEM)
PARAMS = pltpu.CompilerParams(vmem_limit_bytes=20 << 20)


def hbm(*dims, dtype=F32):
    return jax.ShapeDtypeStruct(dims, dtype)


def vmem(*dims, dtype=F32):
    return pltpu.VMEM(dims, dtype)


def call(kernel, outs, args, scratch=()):
    scalar = [a.dtype == jnp.int32 for a in args]
    args = [a if one else pltpu.with_memory_space_constraint(a, pltpu.VMEM) for a, one in zip(args, scalar)]
    return pl.pallas_call(
        kernel,
        out_shape=outs,
        in_specs=[SMEM if one else VMEM for one in scalar],
        out_specs=jax.tree.map(lambda _: VMEM, outs, is_leaf=lambda o: not isinstance(o, tuple)),
        scratch_shapes=scratch,
        compiler_params=PARAMS,
    )(*args)


def local(inverses, couplings, rhs, previous, slot_layer):
    inv, rhs, prev = inverses[0, 0], rhs[0, 0], previous[0, 0]
    place = lax.axis_index("sweep")
    core = (place % 2).reshape(1).astype(jnp.int32)
    group = (place // (2 * RUN)).reshape(1).astype(jnp.int32)
    n_sweep, n_span = lax.axis_size("sweep"), lax.axis_size("span")
    swap = [(i, i ^ 1) for i in range(n_sweep)]
    wide = pltpu.VMEM((2, SECOND, 2 * LANE), F32)

    lower = lax.ppermute(prev, "span", [(i, (i + 1) % n_span) for i in range(n_span)])
    upper = lax.ppermute(prev, "span", [((i + 1) % n_span, i) for i in range(n_span)])
    down = lax.ppermute(prev, "sweep", [(i + 1, i) for i in range(n_sweep - 1)])

    anywhere = pl.BlockSpec(memory_space=pl.ANY)
    whole = [pltpu.with_memory_space_constraint(a, pltpu.HBM) for a in (slot_layer, inv, couplings, rhs, prev)]
    inv, c1, transfer, send, partial = pl.pallas_call(
        local_kernel,
        out_shape=(
            vmem(NZ, BS, BS, dtype=BF16),
            vmem(NZ, BS, BS, dtype=BF16),
            vmem(NZ, ROWS, 2 * LANE),
            hbm(HALF, ROWS, 2 * LANE),
            vmem(NZ, BS, NRHS),
        ),
        in_specs=[SMEM] + [anywhere] * 5,
        out_specs=(VMEM,) * 5,
        scratch_shapes=[
            pltpu.SMEM((1, 1, NZ), jnp.int32),
            pltpu.VMEM((NZ, BS, BS), BF16),
            pltpu.VMEM((2, NZ, BS, BS), BF16),
            pltpu.VMEM((NZ, BS, NRHS), BF16),
            pltpu.VMEM((NZ, BS, NRHS), BF16),
            pltpu.SemaphoreType.DMA((8,)),
        ],
        name="local_kernel",
        compiler_params=PARAMS,
    )(core, *whole)
    sib = lax.ppermute(send, "sweep", swap)
    packed = call(product_kernel, vmem(HALF, PACKED, LANE, dtype=BF16), [core, transfer, sib], [wide])
    partial = pl.pallas_call(
        span_kernel,
        out_shape=vmem(NZ, BS, NRHS),
        in_specs=[anywhere] + [VMEM] * 3,
        out_specs=VMEM,
        scratch_shapes=[pltpu.VMEM((2, NZ, BS, BS), BF16), pltpu.SemaphoreType.DMA((2,))],
        name="span_kernel",
        compiler_params=PARAMS,
    )(whole[2], *(pltpu.with_memory_space_constraint(a, pltpu.VMEM) for a in (partial, lower, upper)))
    offset, send = call(
        offset_kernel,
        (vmem(NZ, BS, NRHS), vmem(HALF, ROWS, NRHS)),
        [core, inv, c1, partial, down],
    )
    offset_sib = lax.ppermute(send, "sweep", swap)
    send = call(
        pair_kernel, vmem(RUN, CHIP, LANE, dtype=BF16), [core, packed, transfer, sib, offset, offset_sib]
    )
    maps = lax.all_to_all(send, "sweep", 0, 0, axis_index_groups=RUNS)
    prefix, shifts, total = call(
        chain_kernel,
        (
            vmem(RUN - 1, 2, BS, BS, dtype=BF16),
            vmem(RUN - 1, BS, NRHS),
            vmem(AFFINE, LANE, dtype=BF16),
        ),
        [maps],
        [pltpu.VMEM((RUN, 2, SECOND, 2 * LANE), BF16), wide],
    )
    totals = lax.all_gather(total, "sweep", axis_index_groups=ACROSS)
    back = call(
        state_kernel,
        vmem(RUN, ROWS, NRHS, dtype=BF16),
        [group, totals, prefix, shifts],
        [pltpu.VMEM((BS, NRHS), F32), pltpu.VMEM((2, SECOND, 2 * LANE), BF16)],
    )
    inflow = lax.all_to_all(back, "sweep", 0, 0, axis_index_groups=RUNS)
    half, send = call(
        half_kernel,
        (vmem(HALF, BS, NRHS), vmem(HALF, ROWS, NRHS, dtype=BF16)),
        [core, transfer, offset, sib, offset_sib, inflow],
    )
    inflow = lax.ppermute(send, "sweep", swap)
    out = call(final_kernel, hbm(NZ * BS, 1, NRHS), [core, transfer, offset, half, inflow])
    return out.reshape(1, 1, NZ, BS, NRHS)


def solution(mesh):
    return jax.shard_map(
        local,
        mesh=mesh,
        in_specs=(
            P("sweep", "span", None, None, None),
            P(None, "sweep", "span", None, None, None),
            P("sweep", "span", None, None, None),
            P("sweep", "span", None, None, None),
            P("sweep", "span", None),
        ),
        out_specs=P("sweep", "span", None, None, None),
        check_vma=False,
    )
```

time: 89.2 us -> 86.6 us (0.971)
  blocking collectives: 37.2 us -> 20.6 us
  waiting for transfers between devices: 8.98 us -> 19.5 us
  starting transfers between devices: 29.2 us -> 36.8 us
  local copies, waits for them, and re-layouts: 5.86 us -> 0.01 us
  Pallas kernels: 6.89 us -> 9.14 us
    all_to_all x2 -> x1, blocking collectives: 37.2 us -> 9.67 us  [local(): inflow = lax.all_to_all(back, 'sweep', 0, 0, axis_index_groups=RUNS)]
    all_gather x0 -> x1, blocking collectives: none -> 10.9 us  [local(): totals = lax.all_gather(total, 'sweep', axis_index_groups=ACROSS)]
    ppermute x3, starting transfers between devices: 11.1 us -> 17.8 us  [the longest x1 8.75 us: local(): sib = lax.ppermute(send, 'sweep', swap)]
    all_to_all x1, waiting for transfers between devices: 7.41 us -> 13.3 us  [local(): maps = lax.all_to_all(send, 'sweep', 0, 0, axis_index_groups=RUNS)]
    all_to_all x1, starting transfers between devices: 3.48 us -> 9.13 us  [local(): maps = lax.all_to_all(send, 'sweep', 0, 0, axis_index_groups=RUNS)]
    pallas_call x0 -> x2, Pallas kernels: none -> 3.54 us  [the longest x1 2.01 us: local(): pl.pallas_call(local_kernel, out_shape=(vmem(NZ, BS, BS, dtype=BF16), vme...]
    ppermute x1, waiting for transfers between devices: 0.01 us -> 2.71 us  [local(): down = lax.ppermute(prev, 'sweep', [(i + 1, i) for i in range(n_sweep - 1)])]
    slice x2 -> x0, local copies, waits for them, and re-layouts: 2.64 us -> none  [the longest x1 1.43 us: local(): faces[1:4]]
  transfers between devices with their start and end apart: 7 -> 7, of which waited for: 3 -> 6; matrix products, arithmetic and copies ran while one was open for 4% -> 0% of each run, Pallas kernels for 4% -> 3%
where the time goes in v3:
time: 86.6 us; the launch traced here: 86.2 us
  starting transfers between devices  36.8 us (42%)
  blocking collectives  20.6 us (24%)
  waiting for transfers between devices  19.5 us (23%)
  Pallas kernels  9.14 us (11%)
    all_to_all x1, waiting for transfers between devices, local(): maps = lax.all_to_all(send, 'sweep', 0, 0, axis_index_groups=RUNS)  13.3 us
    all_gather x1, blocking collectives, local(): totals = lax.all_gather(total, 'sweep', axis_index_groups=ACROSS)  10.9 us
    all_to_all x1, blocking collectives, local(): inflow = lax.all_to_all(back, 'sweep', 0, 0, axis_index_groups=RUNS)  9.67 us
    all_to_all x1, starting transfers between devices, local(): maps = lax.all_to_all(send, 'sweep', 0, 0, axis_index_groups=RUNS)  9.13 us
    ppermute x1, starting transfers between devices, local(): sib = lax.ppermute(send, 'sweep', swap)  8.75 us
    ppermute x1, starting transfers between devices, local(): inflow = lax.ppermute(send, 'sweep', swap)  7.18 us
    pallas_call x7, Pallas kernels, call(): pl.pallas_call(kernel, out_shape=outs, in_specs=[SMEM if one else VMEM fo...  5.6 us
    ppermute x1, starting transfers between devices, local(): lax.ppermute(prev, 'span', [((i + 1) % n_span, i) for i in range(n_span)])  5.47 us
  transfers between devices with their start and end apart: 7, of which 6 were waited for; matrix products, arithmetic and copies ran while one was open for 0% of the time, Pallas kernels for 3%

profile of v3, /device:TPU:1, one launch (start us, length us, event | category | flops | bytes accessed | tf_op | source)
XLA Modules:
  0.0 86.2 jit_solution(11425035710113850841)
XLA Ops:
  0.0 0.0 copy-start
  0.0 2.0 %local_kernel.1 = (bf16[6,135,135]{2,1,0:T(8,128)(2,1)S(1)}, bf16[6,135,135]{2,1,0:T(8,128)(2,1)S(1)}, f32[6,136,256]{2,1,0:T(8,128)S(1)}, f32[3,136,256]{2,1,0:T(8,128)S(1)}, f32[6,135,128]{2,1,0:T(8,128)S(1)}) custom-call(s32[1]{0:T(128)} %bitcast.core, s32[1,1,6]{2,1,0:T(1,128)} %layers_in.1, bf16[6,135,135]{2,1,0:T(8,128)(2,1)} %bitcast.10, ...), custom_call_target="tpu_custom_call" | custom-call | tf_op jit(solution)/shard_map/local_kernel/pallas_call | solution.py:273
  2.0 8.7 %collective-permute-start.3 = (f32[3,136,256]{2,1,0:T(8,128)S(1)}, f32[3,136,256]{2,1,0:T(8,128)S(1)}, u32[]{:S(2)}, u32[]{:S(2)}) collective-permute-start(f32[3,136,256]{2,1,0:T(8,128)S(1)} %get-tuple-element.22), channel_id=1, source_target_pairs={{0,16},{16,0},{32,48},{48,32},{64,80},{80,64},{96,112},{112,96},{1... | collective-permute-start | bytes 1253384 | tf_op jit(solution)/shard_map/ppermute | solution.py:295
  10.8 0.0 copy-done
  10.8 1.9 %collective-permute-start = (bf16[6,135,128]{2,1,0:T(8,128)(2,1)S(1)}, bf16[6,135,128]{2,1,0:T(8,128)(2,1)S(1)}, u32[]{:S(2)}, u32[]{:S(2)}) collective-permute-start(bf16[6,135,128]{2,1,0:T(8,128)(2,1)S(1)} %bitcast.13), channel_id=1, source_target_pairs={{0,1},{1,2},{2,3},{3,4},{4,5},{5,6},{6,7},{7,8},{8,9},{9,10},{10,1... | collective-permute-start | bytes 622088 | tf_op jit(solution)/shard_map/ppermute | solution.py:267
  12.7 5.5 %collective-permute-start.1 = (bf16[6,135,128]{2,1,0:T(8,128)(2,1)S(1)}, bf16[6,135,128]{2,1,0:T(8,128)(2,1)S(1)}, u32[]{:S(2)}, u32[]{:S(2)}) collective-permute-start(bf16[6,135,128]{2,1,0:T(8,128)(2,1)S(1)} %bitcast.14), channel_id=1, source_target_pairs={{1,0},{2,1},{3,2},{4,3},{5,4},{6,5},{7,6},{8,7},{9,8},{10,9},{11,1... | collective-permute-start | bytes 622088 | tf_op jit(solution)/shard_map/ppermute | solution.py:268
  18.2 2.5 %collective-permute-start.2 = (bf16[6,135,128]{2,1,0:T(8,128)(2,1)S(1)}, bf16[6,135,128]{2,1,0:T(8,128)(2,1)S(1)}, u32[]{:S(2)}, u32[]{:S(2)}) collective-permute-start(bf16[6,135,128]{2,1,0:T(8,128)(2,1)S(1)} %bitcast.15), channel_id=1, source_target_pairs={{16,0},{32,16},{48,32},{64,48},{80,64},{96,80},{112,96},{128,112},... | collective-permute-start | bytes 622088 | tf_op jit(solution)/shard_map/ppermute | solution.py:269
  20.7 0.8 collective-permute-done.lower
  21.5 0.9 %collective-permute-done.1.upper = bf16[6,135,128]{2,1,0:T(8,128)(2,1)S(1)} collective-permute-done((bf16[6,135,128]{2,1,0:T(8,128)(2,1)S(1)}, bf16[6,135,128]{2,1,0:T(8,128)(2,1)S(1)}, u32[]{:S(2)}, u32[]{:S(2)}) %collective-permute-start.1) | collective-permute-done | bytes 207392 | tf_op jit(solution)/shard_map/ppermute | solution.py:268
  22.4 1.5 %span_kernel.1.partial = f32[6,135,128]{2,1,0:T(8,128)S(1)} custom-call(bf16[6,1,1,6,135,135]{5,4,3,2,1,0:T(8,128)(2,1)} %c_in.3, f32[6,135,128]{2,1,0:T(8,128)S(1)} %get-tuple-element.20.partial, bf16[6,135,128]{2,1,0:T(8,128)(2,1)S(1)} %collective-permute-done.lower, bf16[6,135,128]{2,1,0:T(8,128)(2,1)S(1)} %collective-permute-done.1.upper), custom_call_target="tpu_custom_call" | custom-call | tf_op jit(solution)/shard_map/span_kernel/pallas_call | solution.py:297
  23.9 2.7 %collective-permute-done.2.down = bf16[6,135,128]{2,1,0:T(8,128)(2,1)S(1)} collective-permute-done((bf16[6,135,128]{2,1,0:T(8,128)(2,1)S(1)}, bf16[6,135,128]{2,1,0:T(8,128)(2,1)S(1)}, u32[]{:S(2)}, u32[]{:S(2)}) %collective-permute-start.2) | collective-permute-done | bytes 207392 | tf_op jit(solution)/shard_map/ppermute | solution.py:269
  26.6 0.5 shard_map.55
  27.2 1.9 %collective-permute-start.4 = (f32[3,136,128]{2,1,0:T(8,128)S(1)}, f32[3,136,128]{2,1,0:T(8,128)S(1)}, u32[]{:S(2)}, u32[]{:S(2)}) collective-permute-start(f32[3,136,128]{2,1,0:T(8,128)S(1)} %get-tuple-element.23), channel_id=1, source_target_pairs={{0,16},{16,0},{32,48},{48,32},{64,80},{80,64},{96,112},{112,96},{1... | collective-permute-start | bytes 626696 | tf_op jit(solution)/shard_map/ppermute | solution.py:311
  29.1 0.0 collective-permute-done.3.sib
  29.1 0.5 shard_map.56.packed
  29.6 0.9 %collective-permute-done.4.offset_sib = f32[3,136,128]{2,1,0:T(8,128)S(1)} collective-permute-done((f32[3,136,128]{2,1,0:T(8,128)S(1)}, f32[3,136,128]{2,1,0:T(8,128)S(1)}, u32[]{:S(2)}, u32[]{:S(2)}) %collective-permute-start.4) | collective-permute-done | bytes 208928 | tf_op jit(solution)/shard_map/ppermute | solution.py:311
  30.5 1.1 %shard_map.57 = bf16[4,456,128]{2,1,0:T(8,128)(2,1)} custom-call(s32[1]{0:T(128)} %bitcast.core, bf16[3,312,128]{2,1,0:T(8,128)(2,1)S(1)} %shard_map.56.packed, f32[6,136,256]{2,1,0:T(8,128)S(1)} %get-tuple-element.17.transfer, f32[3,136,256]{2,1,0:T(8,128)S(1)} %collective-permute-done.3.sib, f32[6,135,128]{2,1,0:T(8,128)S(1)} %get-tuple-element.21.offset, ...), custom_call_target="tpu_custom_call" | custom-call | tf_op jit(solution)/shard_map/pallas_call | solution.py:248
  31.7 9.1 %all-to-all-start = ((bf16[4,456,128]{2,1,0:T(8,128)(2,1)}), bf16[4,456,128]{2,1,0:T(8,128)(2,1)S(1)}, u32[]{:S(2)}, u32[]{:S(2)}) async-start(bf16[4,456,128]{2,1,0:T(8,128)(2,1)} %shard_map.57), calls=%async_computation | async-start | bytes 933888 | tf_op jit(solution)/shard_map/all_to_all | solution.py:315
  40.8 13.3 %all-to-all-done.recv = bf16[4,456,128]{2,1,0:T(8,128)(2,1)S(1)} async-done(((bf16[4,456,128]{2,1,0:T(8,128)(2,1)}), bf16[4,456,128]{2,1,0:T(8,128)(2,1)S(1)}, u32[]{:S(2)}, u32[]{:S(2)}) %all-to-all-start) | async-done | bytes 466976 | tf_op jit(solution)/shard_map/all_to_all | solution.py:315
  54.1 1.0 %shard_map.58 = (bf16[3,2,135,135]{3,2,1,0:T(8,128)(2,1)S(1)}, f32[3,135,128]{2,1,0:T(8,128)S(1)}, bf16[600,128]{1,0:T(8,128)(2,1)S(1)}) custom-call(bf16[4,456,128]{2,1,0:T(8,128)(2,1)S(1)} %all-to-all-done.recv), custom_call_target="tpu_custom_call" | custom-call | tf_op jit(solution)/shard_map/pallas_call | solution.py:248
  55.1 10.9 %all-gather = bf16[2400,128]{1,0:T(8,128)(2,1)S(1)} all-gather(bf16[600,128]{1,0:T(8,128)(2,1)S(1)} %get-tuple-element.24), channel_id=2, replica_groups={{0,128,256,384},{16,144,272,400},{32,160,288,416},{48,176,304,432},{64,..., dimensions={0}, use_global_device_ids=true | all-gather | bytes 768000 | tf_op jit(solution)/shard_map/all_gather | solution.py:326
  66.0 0.3 shard_map.59
  66.4 9.7 %all_to_all.10.inflow = bf16[4,136,128]{2,1,0:T(8,128)(2,1)S(1)} all-to-all(bf16[4,136,128]{2,1,0:T(8,128)(2,1)S(1)} %shard_map.59), channel_id=1, replica_groups={{0,32,64,96},{16,48,80,112},{128,160,192,224},{144,176,208,240},{256,28..., dimensions={0} | all-to-all | bytes 278528 | tf_op jit(solution)/shard_map/all_to_all | solution.py:333
  76.0 0.9 %shard_map.60 = (f32[3,135,128]{2,1,0:T(8,128)S(1)}, bf16[3,136,128]{2,1,0:T(8,128)(2,1)S(1)}) custom-call(s32[1]{0:T(128)} %bitcast.core, f32[6,136,256]{2,1,0:T(8,128)S(1)} %get-tuple-element.17.transfer, f32[6,135,128]{2,1,0:T(8,128)S(1)} %get-tuple-element.21.offset, f32[3,136,256]{2,1,0:T(8,128)S(1)} %collective-permute-done.3.sib, ...), custom_call_target="tpu_custom_call" | custom-call | tf_op jit(solution)/shard_map/pallas_call | solution.py:248
  77.0 7.2 %collective-permute-start.5 = (bf16[3,136,128]{2,1,0:T(8,128)(2,1)S(1)}, bf16[3,136,128]{2,1,0:T(8,128)(2,1)S(1)}, u32[]{:S(2)}, u32[]{:S(2)}) collective-permute-start(bf16[3,136,128]{2,1,0:T(8,128)(2,1)S(1)} %get-tuple-element.28), channel_id=1, source_target_pairs={{0,16},{16,0},{32,48},{48,32},{64,80},{80,64},{96,112},{112,96},{1... | collective-permute-start | bytes 313352 | tf_op jit(solution)/shard_map/ppermute | solution.py:339
  84.1 0.9 %collective-permute-done.5.inflow = bf16[3,136,128]{2,1,0:T(8,128)(2,1)S(1)} collective-permute-done((bf16[3,136,128]{2,1,0:T(8,128)(2,1)S(1)}, bf16[3,136,128]{2,1,0:T(8,128)(2,1)S(1)}, u32[]{:S(2)}, u32[]{:S(2)}) %collective-permute-start.5) | collective-permute-done | bytes 104480 | tf_op jit(solution)/shard_map/ppermute | solution.py:339
  85.1 1.1 %shard_map.61 = f32[810,1,128]{2,1,0:T(1,128)} custom-call(s32[1]{0:T(128)} %bitcast.core, f32[6,136,256]{2,1,0:T(8,128)S(1)} %get-tuple-element.17.transfer, f32[6,135,128]{2,1,0:T(8,128)S(1)} %get-tuple-element.21.offset, f32[3,135,128]{2,1,0:T(8,128)S(1)} %get-tuple-element.27.half, bf16[3,136,128]{2,1,0:T(8,128)(2,1)S(1)} %collective-permute-done.5.inflow), custom_call_target="tpu_custom_call" | custom-call | tf_op jit(solution)/shard_map/pallas_call | solution.py:248
Async XLA Ops:
  0.0 10.8 %copy-start = (bf16[1,1,6,135,128]{4,3,2,1,0:T(8,128)(2,1)S(1)}, bf16[1,1,6,135,128]{4,3,2,1,0:T(8,128)(2,1)}, u32[]{:S(2)}) copy-start(bf16[1,1,6,135,128]{4,3,2,1,0:T(8,128)(2,1)} %param.8) | copy-start | bytes 622084
  2.0 27.1 %collective-permute-start.3 = (f32[3,136,256]{2,1,0:T(8,128)S(1)}, f32[3,136,256]{2,1,0:T(8,128)S(1)}, u32[]{:S(2)}, u32[]{:S(2)}) collective-permute-start(f32[3,136,256]{2,1,0:T(8,128)S(1)} %get-tuple-element.22), channel_id=1, source_target_pairs={{0,16},{16,0},{32,48},{48,32},{64,80},{80,64},{96,112},{112,96},{1... | collective-permute-start | bytes 1253384 | tf_op jit(solution)/shard_map/ppermute | solution.py:295
  10.8 10.7 %collective-permute-start = (bf16[6,135,128]{2,1,0:T(8,128)(2,1)S(1)}, bf16[6,135,128]{2,1,0:T(8,128)(2,1)S(1)}, u32[]{:S(2)}, u32[]{:S(2)}) collective-permute-start(bf16[6,135,128]{2,1,0:T(8,128)(2,1)S(1)} %bitcast.13), channel_id=1, source_target_pairs={{0,1},{1,2},{2,3},{3,4},{4,5},{5,6},{6,7},{7,8},{8,9},{9,10},{10,1... | collective-permute-start | bytes 622088 | tf_op jit(solution)/shard_map/ppermute | solution.py:267
  12.7 9.7 %collective-permute-start.1 = (bf16[6,135,128]{2,1,0:T(8,128)(2,1)S(1)}, bf16[6,135,128]{2,1,0:T(8,128)(2,1)S(1)}, u32[]{:S(2)}, u32[]{:S(2)}) collective-permute-start(bf16[6,135,128]{2,1,0:T(8,128)(2,1)S(1)} %bitcast.14), channel_id=1, source_target_pairs={{1,0},{2,1},{3,2},{4,3},{5,4},{6,5},{7,6},{8,7},{9,8},{10,9},{11,1... | collective-permute-start | bytes 622088 | tf_op jit(solution)/shard_map/ppermute | solution.py:268
  18.2 8.4 %collective-permute-start.2 = (bf16[6,135,128]{2,1,0:T(8,128)(2,1)S(1)}, bf16[6,135,128]{2,1,0:T(8,128)(2,1)S(1)}, u32[]{:S(2)}, u32[]{:S(2)}) collective-permute-start(bf16[6,135,128]{2,1,0:T(8,128)(2,1)S(1)} %bitcast.15), channel_id=1, source_target_pairs={{16,0},{32,16},{48,32},{64,48},{80,64},{96,80},{112,96},{128,112},... | collective-permute-start | bytes 622088 | tf_op jit(solution)/shard_map/ppermute | solution.py:269
  27.2 3.4 %collective-permute-start.4 = (f32[3,136,128]{2,1,0:T(8,128)S(1)}, f32[3,136,128]{2,1,0:T(8,128)S(1)}, u32[]{:S(2)}, u32[]{:S(2)}) collective-permute-start(f32[3,136,128]{2,1,0:T(8,128)S(1)} %get-tuple-element.23), channel_id=1, source_target_pairs={{0,16},{16,0},{32,48},{48,32},{64,80},{80,64},{96,112},{112,96},{1... | collective-permute-start | bytes 626696 | tf_op jit(solution)/shard_map/ppermute | solution.py:311
  31.7 22.4 %all-to-all-start = ((bf16[4,456,128]{2,1,0:T(8,128)(2,1)}), bf16[4,456,128]{2,1,0:T(8,128)(2,1)S(1)}, u32[]{:S(2)}, u32[]{:S(2)}) async-start(bf16[4,456,128]{2,1,0:T(8,128)(2,1)} %shard_map.57), calls=%async_computation | async-start | bytes 933888 | tf_op jit(solution)/shard_map/all_to_all | solution.py:315
  77.0 8.1 %collective-permute-start.5 = (bf16[3,136,128]{2,1,0:T(8,128)(2,1)S(1)}, bf16[3,136,128]{2,1,0:T(8,128)(2,1)S(1)}, u32[]{:S(2)}, u32[]{:S(2)}) collective-permute-start(bf16[3,136,128]{2,1,0:T(8,128)(2,1)S(1)} %get-tuple-element.28), channel_id=1, source_target_pairs={{0,16},{16,0},{32,48},{48,32},{64,80},{80,64},{96,112},{112,96},{1... | collective-permute-start | bytes 313352 | tf_op jit(solution)/shard_map/ppermute | solution.py:339

commit v4 on v3

--- a/solution.py
+++ b/solution.py
@@ -70,7 +70,7 @@
     return ref[at + (slice(SHIFT, SHIFT + BS),)].astype(F32) + ref[at + (slice(LOW, LOW + BS),)].astype(F32)
 
 
-def local_kernel(core, layers_in, inv_in, c_in, rhs_in, prev_in, inv, c1, transfer, send, partial, layers, c0, walls, rhs, prev, sems):
+def local_kernel(place, layers_in, inv_in, c_in, rhs_in, prev_in, inv, c1, transfer, send, partial, layers, c0, walls, rhs, prev, sems):
     moves = (
         (inv_in, inv),
         (c_in.at[0, 0, 0], c0),
@@ -88,7 +88,7 @@
         copy.wait()
     for s in range(NZ):
         transfer[s, :BS, :BS] = -mm(inv[s], c0[s])
-    other = HALF * (1 - core[0])
+    other = HALF * (1 - place[0] % 2)
     for j in range(HALF):
         send[j] = transfer[other + j]
     for copy in copies[2:7]:
@@ -110,8 +110,8 @@
         copy.wait()
 
 
-def product_kernel(core, transfer, sib, packed, wide):
-    c = core[0]
+def product_kernel(place, transfer, sib, packed, wide):
+    c = place[0] % 2
     wide[...] = jnp.zeros_like(wide)
 
     def body(mine):
@@ -127,23 +127,25 @@
     copies = [pltpu.make_async_copy(c_in.at[2 + i, 0, 0], c.at[i], sems.at[i]) for i in range(2)]
     for copy in copies:
         copy.start()
-    for copy in copies:
-        copy.wait()
-    for s in range(NZ):
-        out[s] = partial[s] - (mm(c[0, s], lower[s]) + mm(c[1, s], upper[s]))
-
-
-def offset_kernel(core, inv, c1, partial, down, out, send):
+    copies[0].wait()
+    for s in range(NZ):
+        out[s] = partial[s] - mm(c[0, s], lower[s])
+    copies[1].wait()
+    for s in range(NZ):
+        out[s] = out[s] - mm(c[1, s], upper[s])
+
+
+def offset_kernel(place, inv, c1, partial, down, out, send):
     for s in range(NZ):
         forcing = (partial[s] - mm(c1[s], down[s])).astype(BF16)
         out[s] = mm(inv[s], forcing)
-    other = HALF * (1 - core[0])
+    other = HALF * (1 - place[0] % 2)
     for j in range(HALF):
         send[j, :BS] = out[other + j]
 
 
-def pair_kernel(core, packed, transfer, sib, offset, offset_sib, send):
-    c = core[0]
+def pair_kernel(place, packed, transfer, sib, offset, offset_sib, send):
+    c = place[0] % 2
     send[HALF] = jnp.zeros_like(send[HALF])
     for j in range(HALF):
         send[j, :PACKED] = packed[j]
@@ -177,7 +179,7 @@
 
 
 def state_kernel(place, totals, prefix, shifts, send, state, mat):
-    x = place[0]
+    x = place[0] // (2 * RUN)
     first = jnp.full((BS, NRHS), x, jnp.int32) > 0
     state[...] = jnp.where(first, unpack_shift(totals, (0,)), 0.0)
     for g in range(1, GROUPS - 1):
@@ -192,29 +194,41 @@
         send[k, :BS] = (mm3((prefix[k - 1, 0], prefix[k - 1, 1]), inflow) + shifts[k - 1]).astype(BF16)
 
 
-def half_kernel(core, transfer, offset, sib, offset_sib, inflow, out, send):
-    c = core[0]
+def relay_kernel(place, transfer, offset, inflow, send):
+    c = place[0] % 2
+
+    @pl.when(c == 0)
+    def _():
+        for j in range(HALF):
+            t, v = split(transfer[j, :BS, :BS]), inflow[j, :BS]
+            send[j, :BS] = (offset[j] + (mm(t[0], v) + mm(t[1], v))).astype(BF16)
+
+    @pl.when(c == 1)
+    def _():
+        for j in range(HALF):
+            send[j, :BS] = inflow[j, :BS]
+
+
+def half_kernel(place, transfer, offset, sib, offset_sib, inflow, out):
+    c = place[0] % 2
 
     def body(mine):
         for j in range(HALF):
             s = mine * HALF + j
-            t, o = split(transfer[s, :BS, :BS]), offset[s]
-            v = inflow[j, :BS]
+            t, v = split(transfer[s, :BS, :BS]), inflow[j, :BS]
             if mine == 0:
-                out[j] = o + (mm(t[0], v) + mm(t[1], v))
-                send[j, :BS] = out[j].astype(BF16)
+                out[j] = offset[s] + (mm(t[0], v) + mm(t[1], v))
             else:
                 first = split(sib[j, :BS, :BS])
                 middle = offset_sib[j, :BS] + (mm(first[0], v) + mm(first[1], v))
-                out[j] = o + mm3(t, split(middle))
-                send[j, :BS] = v
+                out[j] = offset[s] + mm3(t, split(middle))
 
     pl.when(c == 0)(lambda: body(0))
     pl.when(c == 1)(lambda: body(1))
 
 
-def final_kernel(core, transfer, offset, half, inflow, out):
-    c = core[0]
+def final_kernel(place, transfer, offset, half, inflow, out):
+    c = place[0] % 2
 
     def body(mine):
         for j in range(HALF):
@@ -257,9 +271,7 @@
 
 def local(inverses, couplings, rhs, previous, slot_layer):
     inv, rhs, prev = inverses[0, 0], rhs[0, 0], previous[0, 0]
-    place = lax.axis_index("sweep")
-    core = (place % 2).reshape(1).astype(jnp.int32)
-    group = (place // (2 * RUN)).reshape(1).astype(jnp.int32)
+    place = lax.axis_index("sweep").reshape(1).astype(jnp.int32)
     n_sweep, n_span = lax.axis_size("sweep"), lax.axis_size("span")
     swap = [(i, i ^ 1) for i in range(n_sweep)]
     wide = pltpu.VMEM((2, SECOND, 2 * LANE), F32)
@@ -291,9 +303,9 @@
         ],
         name="local_kernel",
         compiler_params=PARAMS,
-    )(core, *whole)
+    )(place, *whole)
     sib = lax.ppermute(send, "sweep", swap)
-    packed = call(product_kernel, vmem(HALF, PACKED, LANE, dtype=BF16), [core, transfer, sib], [wide])
+    packed = call(product_kernel, vmem(HALF, PACKED, LANE, dtype=BF16), [place, transfer, sib], [wide])
     partial = pl.pallas_call(
         span_kernel,
         out_shape=vmem(NZ, BS, NRHS),
@@ -306,11 +318,11 @@
     offset, send = call(
         offset_kernel,
         (vmem(NZ, BS, NRHS), vmem(HALF, ROWS, NRHS)),
-        [core, inv, c1, partial, down],
+        [place, inv, c1, partial, down],
     )
     offset_sib = lax.ppermute(send, "sweep", swap)
     send = call(
-        pair_kernel, vmem(RUN, CHIP, LANE, dtype=BF16), [core, packed, transfer, sib, offset, offset_sib]
+        pair_kernel, vmem(RUN, CHIP, LANE, dtype=BF16), [place, packed, transfer, sib, offset, offset_sib]
     )
     maps = lax.all_to_all(send, "sweep", 0, 0, axis_index_groups=RUNS)
     prefix, shifts, total = call(
@@ -327,17 +339,14 @@
     back = call(
         state_kernel,
         vmem(RUN, ROWS, NRHS, dtype=BF16),
-        [group, totals, prefix, shifts],
+        [place, totals, prefix, shifts],
         [pltpu.VMEM((BS, NRHS), F32), pltpu.VMEM((2, SECOND, 2 * LANE), BF16)],
     )
     inflow = lax.all_to_all(back, "sweep", 0, 0, axis_index_groups=RUNS)
-    half, send = call(
-        half_kernel,
-        (vmem(HALF, BS, NRHS), vmem(HALF, ROWS, NRHS, dtype=BF16)),
-        [core, transfer, offset, sib, offset_sib, inflow],
-    )
+    send = call(relay_kernel, vmem(HALF, ROWS, NRHS, dtype=BF16), [place, transfer, offset, inflow])
+    half = call(half_kernel, vmem(HALF, BS, NRHS), [place, transfer, offset, sib, offset_sib, inflow])
     inflow = lax.ppermute(send, "sweep", swap)
-    out = call(final_kernel, hbm(NZ * BS, 1, NRHS), [core, transfer, offset, half, inflow])
+    out = call(final_kernel, hbm(NZ * BS, 1, NRHS), [place, transfer, offset, half, inflow])
     return out.reshape(1, 1, NZ, BS, NRHS)
 
 

time: 86.6 us -> 86.2 us (level)
  blocking collectives: 20.6 us -> 43.7 us
  waiting for transfers between devices: 19.5 us -> 5.28 us
  starting transfers between devices: 36.8 us -> 28.3 us
    all_to_all x0 -> x1, blocking collectives: none -> 22 us  [local(): maps = lax.all_to_all(send, 'sweep', 0, 0, axis_index_groups=RUNS)]
    all_to_all x1 -> x0, waiting for transfers between devices: 13.3 us -> none  [local(): maps = lax.all_to_all(send, 'sweep', 0, 0, axis_index_groups=RUNS)]
    all_to_all x1 -> x0, starting transfers between devices: 9.13 us -> none  [local(): maps = lax.all_to_all(send, 'sweep', 0, 0, axis_index_groups=RUNS)]
    ppermute x1, waiting for transfers between devices: 0.93 us -> 0.01 us  [local(): inflow = lax.ppermute(send, 'sweep', swap)]
    pallas_call x7 -> x8, Pallas kernels: 5.6 us -> 4.89 us  [call(): pl.pallas_call(kernel, out_shape=outs, in_specs=[SMEM if one else VMEM fo...]
  transfers between devices with their start and end apart: 7 -> 6, of which waited for: 6 -> 4; matrix products, arithmetic and copies ran while one was open for 0% -> 0% of each run, Pallas kernels for 3% -> 4%
where the time goes in v4:
time: 86.2 us; the launch traced here: 85.9 us
  blocking collectives  43.7 us (51%)
  starting transfers between devices  28.3 us (33%)
  Pallas kernels  8.45 us (10%)
  waiting for transfers between devices  5.28 us (6%)
    all_to_all x1, blocking collectives, local(): maps = lax.all_to_all(send, 'sweep', 0, 0, axis_index_groups=RUNS)  22 us
    all_gather x1, blocking collectives, local(): totals = lax.all_gather(total, 'sweep', axis_index_groups=ACROSS)  11.5 us
    all_to_all x1, blocking collectives, local(): inflow = lax.all_to_all(back, 'sweep', 0, 0, axis_index_groups=RUNS)  10.1 us
    ppermute x1, starting transfers between devices, local(): sib = lax.ppermute(send, 'sweep', swap)  8.75 us
    ppermute x1, starting transfers between devices, local(): inflow = lax.ppermute(send, 'sweep', swap)  7.75 us
    ppermute x1, starting transfers between devices, local(): lax.ppermute(prev, 'span', [((i + 1) % n_span, i) for i in range(n_span)])  5.47 us
    pallas_call x8, Pallas kernels, call(): pl.pallas_call(kernel, out_shape=outs, in_specs=[SMEM if one else VMEM fo...  4.89 us
    ppermute x1, waiting for transfers between devices, local(): down = lax.ppermute(prev, 'sweep', [(i + 1, i) for i in range(n_sweep - 1)])  2.68 us
  transfers between devices with their start and end apart: 6, of which 4 were waited for; matrix products, arithmetic and copies ran while one was open for 0% of the time, Pallas kernels for 4%

profile of v4, /device:TPU:1, one launch (start us, length us, event | category | flops | bytes accessed | tf_op | source)
XLA Modules:
  0.0 85.9 jit_solution(6919356711730572683)
XLA Ops:
  0.0 0.0 copy-start
  0.0 2.0 %local_kernel.1 = (bf16[6,135,135]{2,1,0:T(8,128)(2,1)S(1)}, bf16[6,135,135]{2,1,0:T(8,128)(2,1)S(1)}, f32[6,136,256]{2,1,0:T(8,128)S(1)}, f32[3,136,256]{2,1,0:T(8,128)S(1)}, f32[6,135,128]{2,1,0:T(8,128)S(1)}) custom-call(s32[1]{0:T(128)} %bitcast.place, s32[1,1,6]{2,1,0:T(1,128)} %layers_in.1, bf16[6,135,135]{2,1,0:T(8,128)(2,1)} %bitcast.9, ...), custom_call_target="tpu_custom_call" | custom-call | tf_op jit(solution)/shard_map/local_kernel/pallas_call | solution.py:285
  2.0 8.7 %collective-permute-start.3 = (f32[3,136,256]{2,1,0:T(8,128)S(1)}, f32[3,136,256]{2,1,0:T(8,128)S(1)}, u32[]{:S(2)}, u32[]{:S(2)}) collective-permute-start(f32[3,136,256]{2,1,0:T(8,128)S(1)} %get-tuple-element.20), channel_id=1, source_target_pairs={{0,16},{16,0},{32,48},{48,32},{64,80},{80,64},{96,112},{112,96},{1... | collective-permute-start | bytes 1253384 | tf_op jit(solution)/shard_map/ppermute | solution.py:307
  10.8 0.0 copy-done
  10.8 1.9 %collective-permute-start = (bf16[6,135,128]{2,1,0:T(8,128)(2,1)S(1)}, bf16[6,135,128]{2,1,0:T(8,128)(2,1)S(1)}, u32[]{:S(2)}, u32[]{:S(2)}) collective-permute-start(bf16[6,135,128]{2,1,0:T(8,128)(2,1)S(1)} %bitcast.12), channel_id=1, source_target_pairs={{0,1},{1,2},{2,3},{3,4},{4,5},{5,6},{6,7},{7,8},{8,9},{9,10},{10,1... | collective-permute-start | bytes 622088 | tf_op jit(solution)/shard_map/ppermute | solution.py:279
  12.7 5.5 %collective-permute-start.1 = (bf16[6,135,128]{2,1,0:T(8,128)(2,1)S(1)}, bf16[6,135,128]{2,1,0:T(8,128)(2,1)S(1)}, u32[]{:S(2)}, u32[]{:S(2)}) collective-permute-start(bf16[6,135,128]{2,1,0:T(8,128)(2,1)S(1)} %bitcast.13), channel_id=1, source_target_pairs={{1,0},{2,1},{3,2},{4,3},{5,4},{6,5},{7,6},{8,7},{9,8},{10,9},{11,1... | collective-permute-start | bytes 622088 | tf_op jit(solution)/shard_map/ppermute | solution.py:280
  18.2 2.5 %collective-permute-start.2 = (bf16[6,135,128]{2,1,0:T(8,128)(2,1)S(1)}, bf16[6,135,128]{2,1,0:T(8,128)(2,1)S(1)}, u32[]{:S(2)}, u32[]{:S(2)}) collective-permute-start(bf16[6,135,128]{2,1,0:T(8,128)(2,1)S(1)} %bitcast.14), channel_id=1, source_target_pairs={{16,0},{32,16},{48,32},{64,48},{80,64},{96,80},{112,96},{128,112},... | collective-permute-start | bytes 622088 | tf_op jit(solution)/shard_map/ppermute | solution.py:281
  20.7 0.8 collective-permute-done.lower
  21.5 0.9 %collective-permute-done.1.upper = bf16[6,135,128]{2,1,0:T(8,128)(2,1)S(1)} collective-permute-done((bf16[6,135,128]{2,1,0:T(8,128)(2,1)S(1)}, bf16[6,135,128]{2,1,0:T(8,128)(2,1)S(1)}, u32[]{:S(2)}, u32[]{:S(2)}) %collective-permute-start.1) | collective-permute-done | bytes 207392 | tf_op jit(solution)/shard_map/ppermute | solution.py:280
  22.4 1.6 %span_kernel.1.partial = f32[6,135,128]{2,1,0:T(8,128)S(1)} custom-call(bf16[6,1,1,6,135,135]{5,4,3,2,1,0:T(8,128)(2,1)} %c_in.3, f32[6,135,128]{2,1,0:T(8,128)S(1)} %get-tuple-element.18.partial, bf16[6,135,128]{2,1,0:T(8,128)(2,1)S(1)} %collective-permute-done.lower, bf16[6,135,128]{2,1,0:T(8,128)(2,1)S(1)} %collective-permute-done.1.upper), custom_call_target="tpu_custom_call" | custom-call | tf_op jit(solution)/shard_map/span_kernel/pallas_call | solution.py:309
  24.0 2.7 %collective-permute-done.2.down = bf16[6,135,128]{2,1,0:T(8,128)(2,1)S(1)} collective-permute-done((bf16[6,135,128]{2,1,0:T(8,128)(2,1)S(1)}, bf16[6,135,128]{2,1,0:T(8,128)(2,1)S(1)}, u32[]{:S(2)}, u32[]{:S(2)}) %collective-permute-start.2) | collective-permute-done | bytes 207392 | tf_op jit(solution)/shard_map/ppermute | solution.py:281
  26.6 0.5 shard_map.55
  27.2 1.9 %collective-permute-start.4 = (f32[3,136,128]{2,1,0:T(8,128)S(1)}, f32[3,136,128]{2,1,0:T(8,128)S(1)}, u32[]{:S(2)}, u32[]{:S(2)}) collective-permute-start(f32[3,136,128]{2,1,0:T(8,128)S(1)} %get-tuple-element.21), channel_id=1, source_target_pairs={{0,16},{16,0},{32,48},{48,32},{64,80},{80,64},{96,112},{112,96},{1... | collective-permute-start | bytes 626696 | tf_op jit(solution)/shard_map/ppermute | solution.py:323
  29.1 0.0 collective-permute-done.3.sib
  29.1 0.5 shard_map.56.packed
  29.7 0.9 %collective-permute-done.4.offset_sib = f32[3,136,128]{2,1,0:T(8,128)S(1)} collective-permute-done((f32[3,136,128]{2,1,0:T(8,128)S(1)}, f32[3,136,128]{2,1,0:T(8,128)S(1)}, u32[]{:S(2)}, u32[]{:S(2)}) %collective-permute-start.4) | collective-permute-done | bytes 208928 | tf_op jit(solution)/shard_map/ppermute | solution.py:323
  30.5 0.4 shard_map.57
  30.9 22.0 %all_to_all.10.recv = bf16[4,456,128]{2,1,0:T(8,128)(2,1)S(1)} all-to-all(bf16[4,456,128]{2,1,0:T(8,128)(2,1)S(1)} %shard_map.57), channel_id=1, replica_groups={{0,32,64,96},{16,48,80,112},{128,160,192,224},{144,176,208,240},{256,28..., dimensions={0} | all-to-all | bytes 933888 | tf_op jit(solution)/shard_map/all_to_all | solution.py:327
  52.9 1.0 %shard_map.58 = (bf16[3,2,135,135]{3,2,1,0:T(8,128)(2,1)S(1)}, f32[3,135,128]{2,1,0:T(8,128)S(1)}, bf16[600,128]{1,0:T(8,128)(2,1)S(1)}) custom-call(bf16[4,456,128]{2,1,0:T(8,128)(2,1)S(1)} %all_to_all.10.recv), custom_call_target="tpu_custom_call" | custom-call | tf_op jit(solution)/shard_map/pallas_call | solution.py:262
  53.9 11.5 %all-gather = bf16[2400,128]{1,0:T(8,128)(2,1)S(1)} all-gather(bf16[600,128]{1,0:T(8,128)(2,1)S(1)} %get-tuple-element.22), channel_id=2, replica_groups={{0,128,256,384},{16,144,272,400},{32,160,288,416},{48,176,304,432},{64,..., dimensions={0}, use_global_device_ids=true | all-gather | bytes 768000 | tf_op jit(solution)/shard_map/all_gather | solution.py:338
  65.5 0.3 shard_map.59
  65.8 10.1 %all_to_all.11.inflow = bf16[4,136,128]{2,1,0:T(8,128)(2,1)S(1)} all-to-all(bf16[4,136,128]{2,1,0:T(8,128)(2,1)S(1)} %shard_map.59), channel_id=1, replica_groups={{0,32,64,96},{16,48,80,112},{128,160,192,224},{144,176,208,240},{256,28..., dimensions={0} | all-to-all | bytes 278528 | tf_op jit(solution)/shard_map/all_to_all | solution.py:345
  76.0 7.8 %collective-permute-start.5 = (bf16[3,136,128]{2,1,0:T(8,128)(2,1)S(1)}, bf16[3,136,128]{2,1,0:T(8,128)(2,1)S(1)}, u32[]{:S(2)}, u32[]{:S(2)}) collective-permute-start(bf16[3,136,128]{2,1,0:T(8,128)(2,1)S(1)} %shard_map.61), channel_id=1, source_target_pairs={{0,16},{16,0},{32,48},{48,32},{64,80},{80,64},{96,112},{112,96},{1... | collective-permute-start | bytes 313352 | tf_op jit(solution)/shard_map/ppermute | solution.py:348
  83.7 0.9 %shard_map.60.half = f32[3,135,128]{2,1,0:T(8,128)S(1)} custom-call(s32[1]{0:T(128)} %bitcast.place, f32[6,136,256]{2,1,0:T(8,128)S(1)} %get-tuple-element.15.transfer, f32[6,135,128]{2,1,0:T(8,128)S(1)} %get-tuple-element.19.offset, f32[3,136,256]{2,1,0:T(8,128)S(1)} %collective-permute-done.3.sib, f32[3,136,128]{2,1,0:T(8,128)S(1)} %collective-permute-done.4.offset_sib, ...), custom_call_target="tpu_custom_call" | custom-call | tf_op jit(solution)/shard_map/pallas_call | solution.py:262
  84.7 0.0 collective-permute-done.5.inflow
  84.7 1.2 %shard_map.62 = f32[810,1,128]{2,1,0:T(1,128)} custom-call(s32[1]{0:T(128)} %bitcast.place, f32[6,136,256]{2,1,0:T(8,128)S(1)} %get-tuple-element.15.transfer, f32[6,135,128]{2,1,0:T(8,128)S(1)} %get-tuple-element.19.offset, f32[3,135,128]{2,1,0:T(8,128)S(1)} %shard_map.60.half, bf16[3,136,128]{2,1,0:T(8,128)(2,1)S(1)} %collective-permute-done.5.inflow), custom_call_target="tpu_custom_call" | custom-call | tf_op jit(solution)/shard_map/pallas_call | solution.py:262
  (1 shorter events, 0.0 us)
Async XLA Ops:
  0.0 10.8 %copy-start = (bf16[1,1,6,135,128]{4,3,2,1,0:T(8,128)(2,1)S(1)}, bf16[1,1,6,135,128]{4,3,2,1,0:T(8,128)(2,1)}, u32[]{:S(2)}) copy-start(bf16[1,1,6,135,128]{4,3,2,1,0:T(8,128)(2,1)} %param.8) | copy-start | bytes 622084
  2.0 27.1 %collective-permute-start.3 = (f32[3,136,256]{2,1,0:T(8,128)S(1)}, f32[3,136,256]{2,1,0:T(8,128)S(1)}, u32[]{:S(2)}, u32[]{:S(2)}) collective-permute-start(f32[3,136,256]{2,1,0:T(8,128)S(1)} %get-tuple-element.20), channel_id=1, source_target_pairs={{0,16},{16,0},{32,48},{48,32},{64,80},{80,64},{96,112},{112,96},{1... | collective-permute-start | bytes 1253384 | tf_op jit(solution)/shard_map/ppermute | solution.py:307
  10.8 10.7 %collective-permute-start = (bf16[6,135,128]{2,1,0:T(8,128)(2,1)S(1)}, bf16[6,135,128]{2,1,0:T(8,128)(2,1)S(1)}, u32[]{:S(2)}, u32[]{:S(2)}) collective-permute-start(bf16[6,135,128]{2,1,0:T(8,128)(2,1)S(1)} %bitcast.12), channel_id=1, source_target_pairs={{0,1},{1,2},{2,3},{3,4},{4,5},{5,6},{6,7},{7,8},{8,9},{9,10},{10,1... | collective-permute-start | bytes 622088 | tf_op jit(solution)/shard_map/ppermute | solution.py:279
  12.7 9.7 %collective-permute-start.1 = (bf16[6,135,128]{2,1,0:T(8,128)(2,1)S(1)}, bf16[6,135,128]{2,1,0:T(8,128)(2,1)S(1)}, u32[]{:S(2)}, u32[]{:S(2)}) collective-permute-start(bf16[6,135,128]{2,1,0:T(8,128)(2,1)S(1)} %bitcast.13), channel_id=1, source_target_pairs={{1,0},{2,1},{3,2},{4,3},{5,4},{6,5},{7,6},{8,7},{9,8},{10,9},{11,1... | collective-permute-start | bytes 622088 | tf_op jit(solution)/shard_map/ppermute | solution.py:280
  18.2 8.4 %collective-permute-start.2 = (bf16[6,135,128]{2,1,0:T(8,128)(2,1)S(1)}, bf16[6,135,128]{2,1,0:T(8,128)(2,1)S(1)}, u32[]{:S(2)}, u32[]{:S(2)}) collective-permute-start(bf16[6,135,128]{2,1,0:T(8,128)(2,1)S(1)} %bitcast.14), channel_id=1, source_target_pairs={{16,0},{32,16},{48,32},{64,48},{80,64},{96,80},{112,96},{128,112},... | collective-permute-start | bytes 622088 | tf_op jit(solution)/shard_map/ppermute | solution.py:281
  27.2 3.4 %collective-permute-start.4 = (f32[3,136,128]{2,1,0:T(8,128)S(1)}, f32[3,136,128]{2,1,0:T(8,128)S(1)}, u32[]{:S(2)}, u32[]{:S(2)}) collective-permute-start(f32[3,136,128]{2,1,0:T(8,128)S(1)} %get-tuple-element.21), channel_id=1, source_target_pairs={{0,16},{16,0},{32,48},{48,32},{64,80},{80,64},{96,112},{112,96},{1... | collective-permute-start | bytes 626696 | tf_op jit(solution)/shard_map/ppermute | solution.py:323
  76.0 8.7 %collective-permute-start.5 = (bf16[3,136,128]{2,1,0:T(8,128)(2,1)S(1)}, bf16[3,136,128]{2,1,0:T(8,128)(2,1)S(1)}, u32[]{:S(2)}, u32[]{:S(2)}) collective-permute-start(bf16[3,136,128]{2,1,0:T(8,128)(2,1)S(1)} %shard_map.61), channel_id=1, source_target_pairs={{0,16},{16,0},{32,48},{48,32},{64,80},{80,64},{96,112},{112,96},{1... | collective-permute-start | bytes 313352 | tf_op jit(solution)/shard_map/ppermute | solution.py:348

commit v5 on v4

--- a/solution.py
+++ b/solution.py
@@ -70,7 +70,7 @@
     return ref[at + (slice(SHIFT, SHIFT + BS),)].astype(F32) + ref[at + (slice(LOW, LOW + BS),)].astype(F32)
 
 
-def local_kernel(place, layers_in, inv_in, c_in, rhs_in, prev_in, inv, c1, transfer, send, partial, layers, c0, walls, rhs, prev, sems):
+def local_kernel(place, layers_in, inv_in, c_in, rhs_in, prev_in, inv, last, transfer, send, partial, layers, c0, walls, rhs, prev, sems):
     moves = (
         (inv_in, inv),
         (c_in.at[0, 0, 0], c0),
@@ -79,7 +79,7 @@
         (layers_in, layers),
         (c_in.at[4, 0, 0], walls.at[0]),
         (c_in.at[5, 0, 0], walls.at[1]),
-        (c_in.at[1, 0, 0], c1),
+        (c_in.at[3, 0, 0], last),
     )
     copies = [pltpu.make_async_copy(source, target, sems.at[i]) for i, (source, target) in enumerate(moves)]
     for copy in copies:
@@ -123,21 +123,21 @@
     pl.when(c == 1)(lambda: body(1))
 
 
-def span_kernel(c_in, partial, lower, upper, out, c, sems):
-    copies = [pltpu.make_async_copy(c_in.at[2 + i, 0, 0], c.at[i], sems.at[i]) for i in range(2)]
+def early_kernel(c_in, partial, down, lower, out, c, sems):
+    copies = [pltpu.make_async_copy(c_in.at[1 + i, 0, 0], c.at[i], sems.at[i]) for i in range(2)]
     for copy in copies:
         copy.start()
     copies[0].wait()
     for s in range(NZ):
-        out[s] = partial[s] - mm(c[0, s], lower[s])
+        out[s] = partial[s] - mm(c[0, s], down[s])
     copies[1].wait()
     for s in range(NZ):
-        out[s] = out[s] - mm(c[1, s], upper[s])
-
-
-def offset_kernel(place, inv, c1, partial, down, out, send):
-    for s in range(NZ):
-        forcing = (partial[s] - mm(c1[s], down[s])).astype(BF16)
+        out[s] = out[s] - mm(c[1, s], lower[s])
+
+
+def offset_kernel(place, inv, c, partial, upper, out, send):
+    for s in range(NZ):
+        forcing = (partial[s] - mm(c[s], upper[s])).astype(BF16)
         out[s] = mm(inv[s], forcing)
     other = HALF * (1 - place[0] % 2)
     for j in range(HALF):
@@ -282,7 +282,7 @@
 
     anywhere = pl.BlockSpec(memory_space=pl.ANY)
     whole = [pltpu.with_memory_space_constraint(a, pltpu.HBM) for a in (slot_layer, inv, couplings, rhs, prev)]
-    inv, c1, transfer, send, partial = pl.pallas_call(
+    inv, last, transfer, send, partial = pl.pallas_call(
         local_kernel,
         out_shape=(
             vmem(NZ, BS, BS, dtype=BF16),
@@ -307,18 +307,18 @@
     sib = lax.ppermute(send, "sweep", swap)
     packed = call(product_kernel, vmem(HALF, PACKED, LANE, dtype=BF16), [place, transfer, sib], [wide])
     partial = pl.pallas_call(
-        span_kernel,
+        early_kernel,
         out_shape=vmem(NZ, BS, NRHS),
         in_specs=[anywhere] + [VMEM] * 3,
         out_specs=VMEM,
         scratch_shapes=[pltpu.VMEM((2, NZ, BS, BS), BF16), pltpu.SemaphoreType.DMA((2,))],
-        name="span_kernel",
+        name="early_kernel",
         compiler_params=PARAMS,
-    )(whole[2], *(pltpu.with_memory_space_constraint(a, pltpu.VMEM) for a in (partial, lower, upper)))
+    )(whole[2], *(pltpu.with_memory_space_constraint(a, pltpu.VMEM) for a in (partial, down, lower)))
     offset, send = call(
         offset_kernel,
         (vmem(NZ, BS, NRHS), vmem(HALF, ROWS, NRHS)),
-        [place, inv, c1, partial, down],
+        [place, inv, last, partial, upper],
     )
     offset_sib = lax.ppermute(send, "sweep", swap)
     send = call(

time: 86.2 us -> 84.4 us (0.979)
  the two profiles are of different devices: /device:TPU:1 before, /device:TPU:31 now
where the time goes in v5:
time: 84.4 us; the launch traced here: 84 us
  blocking collectives  37.6 us (45%)
  starting transfers between devices  32.5 us (39%)
  Pallas kernels  8.99 us (11%)
  waiting for transfers between devices  4.79 us (6%)
    all_to_all x1, blocking collectives, local(): maps = lax.all_to_all(send, 'sweep', 0, 0, axis_index_groups=RUNS)  14.8 us
    ppermute x1, starting transfers between devices, local(): offset_sib = lax.ppermute(send, 'sweep', swap)  12.8 us
    all_to_all x1, blocking collectives, local(): inflow = lax.all_to_all(back, 'sweep', 0, 0, axis_index_groups=RUNS)  11.6 us
    all_gather x1, blocking collectives, local(): totals = lax.all_gather(total, 'sweep', axis_index_groups=ACROSS)  11.1 us
    ppermute x1, starting transfers between devices, local(): inflow = lax.ppermute(send, 'sweep', swap)  8.89 us
    pallas_call x8, Pallas kernels, call(): pl.pallas_call(kernel, out_shape=outs, in_specs=[SMEM if one else VMEM fo...  5.43 us
    ppermute x1, starting transfers between devices, local(): lax.ppermute(prev, 'span', [(i, (i + 1) % n_span) for i in range(n_span)])  4.41 us
    ppermute x1, waiting for transfers between devices, local(): down = lax.ppermute(prev, 'sweep', [(i + 1, i) for i in range(n_sweep - 1)])  3.15 us
  transfers between devices with their start and end apart: 6, of which 3 were waited for; matrix products, arithmetic and copies ran while one was open for 0% of the time, Pallas kernels for 4%

profile of v5, /device:TPU:31, one launch (start us, length us, event | category | flops | bytes accessed | tf_op | source)
XLA Modules:
  0.0 84.0 jit_solution(4543842811678819081)
XLA Ops:
  0.0 0.0 copy-start
  0.0 2.0 %local_kernel.1 = (bf16[6,135,135]{2,1,0:T(8,128)(2,1)S(1)}, bf16[6,135,135]{2,1,0:T(8,128)(2,1)S(1)}, f32[6,136,256]{2,1,0:T(8,128)S(1)}, f32[3,136,256]{2,1,0:T(8,128)S(1)}, f32[6,135,128]{2,1,0:T(8,128)S(1)}) custom-call(s32[1]{0:T(128)} %bitcast.place, s32[1,1,6]{2,1,0:T(1,128)} %layers_in.1, bf16[6,135,135]{2,1,0:T(8,128)(2,1)} %bitcast.9, ...), custom_call_target="tpu_custom_call" | custom-call | tf_op jit(solution)/shard_map/local_kernel/pallas_call | solution.py:285
  2.0 2.6 %collective-permute-start.3 = (f32[3,136,256]{2,1,0:T(8,128)S(1)}, f32[3,136,256]{2,1,0:T(8,128)S(1)}, u32[]{:S(2)}, u32[]{:S(2)}) collective-permute-start(f32[3,136,256]{2,1,0:T(8,128)S(1)} %get-tuple-element.20), channel_id=1, source_target_pairs={{0,16},{16,0},{32,48},{48,32},{64,80},{80,64},{96,112},{112,96},{1... | collective-permute-start | bytes 1253384 | tf_op jit(solution)/shard_map/ppermute | solution.py:307
  4.6 0.0 copy-done
  4.6 1.9 %collective-permute-start = (bf16[6,135,128]{2,1,0:T(8,128)(2,1)S(1)}, bf16[6,135,128]{2,1,0:T(8,128)(2,1)S(1)}, u32[]{:S(2)}, u32[]{:S(2)}) collective-permute-start(bf16[6,135,128]{2,1,0:T(8,128)(2,1)S(1)} %bitcast.12), channel_id=1, source_target_pairs={{16,0},{32,16},{48,32},{64,48},{80,64},{96,80},{112,96},{128,112},... | collective-permute-start | bytes 622088 | tf_op jit(solution)/shard_map/ppermute | solution.py:281
  6.6 4.4 %collective-permute-start.1 = (bf16[6,135,128]{2,1,0:T(8,128)(2,1)S(1)}, bf16[6,135,128]{2,1,0:T(8,128)(2,1)S(1)}, u32[]{:S(2)}, u32[]{:S(2)}) collective-permute-start(bf16[6,135,128]{2,1,0:T(8,128)(2,1)S(1)} %bitcast.13), channel_id=1, source_target_pairs={{0,1},{1,2},{2,3},{3,4},{4,5},{5,6},{6,7},{7,8},{8,9},{9,10},{10,1... | collective-permute-start | bytes 622088 | tf_op jit(solution)/shard_map/ppermute | solution.py:279
  11.0 1.9 %collective-permute-start.2 = (bf16[6,135,128]{2,1,0:T(8,128)(2,1)S(1)}, bf16[6,135,128]{2,1,0:T(8,128)(2,1)S(1)}, u32[]{:S(2)}, u32[]{:S(2)}) collective-permute-start(bf16[6,135,128]{2,1,0:T(8,128)(2,1)S(1)} %bitcast.14), channel_id=1, source_target_pairs={{1,0},{2,1},{3,2},{4,3},{5,4},{6,5},{7,6},{8,7},{9,8},{10,9},{11,1... | collective-permute-start | bytes 622088 | tf_op jit(solution)/shard_map/ppermute | solution.py:280
  12.9 3.1 %collective-permute-done.down = bf16[6,135,128]{2,1,0:T(8,128)(2,1)S(1)} collective-permute-done((bf16[6,135,128]{2,1,0:T(8,128)(2,1)S(1)}, bf16[6,135,128]{2,1,0:T(8,128)(2,1)S(1)}, u32[]{:S(2)}, u32[]{:S(2)}) %collective-permute-start) | collective-permute-done | bytes 207392 | tf_op jit(solution)/shard_map/ppermute | solution.py:281
  16.1 0.0 collective-permute-done.1.lower
  16.1 1.6 %early_kernel.1.partial = f32[6,135,128]{2,1,0:T(8,128)S(1)} custom-call(bf16[6,1,1,6,135,135]{5,4,3,2,1,0:T(8,128)(2,1)} %c_in.3, f32[6,135,128]{2,1,0:T(8,128)S(1)} %get-tuple-element.18.partial, bf16[6,135,128]{2,1,0:T(8,128)(2,1)S(1)} %collective-permute-done.down, bf16[6,135,128]{2,1,0:T(8,128)(2,1)S(1)} %collective-permute-done.1.lower), custom_call_target="tpu_custom_call" | custom-call | tf_op jit(solution)/shard_map/early_kernel/pallas_call | solution.py:309
  17.6 1.1 %collective-permute-done.2.upper = bf16[6,135,128]{2,1,0:T(8,128)(2,1)S(1)} collective-permute-done((bf16[6,135,128]{2,1,0:T(8,128)(2,1)S(1)}, bf16[6,135,128]{2,1,0:T(8,128)(2,1)S(1)}, u32[]{:S(2)}, u32[]{:S(2)}) %collective-permute-start.2) | collective-permute-done | bytes 207392 | tf_op jit(solution)/shard_map/ppermute | solution.py:280
  18.7 0.5 shard_map.55
  19.3 12.8 %collective-permute-start.4 = (f32[3,136,128]{2,1,0:T(8,128)S(1)}, f32[3,136,128]{2,1,0:T(8,128)S(1)}, u32[]{:S(2)}, u32[]{:S(2)}) collective-permute-start(f32[3,136,128]{2,1,0:T(8,128)S(1)} %get-tuple-element.21), channel_id=1, source_target_pairs={{0,16},{16,0},{32,48},{48,32},{64,80},{80,64},{96,112},{112,96},{1... | collective-permute-start | bytes 626696 | tf_op jit(solution)/shard_map/ppermute | solution.py:323
  32.1 0.0 collective-permute-done.3.sib
  32.1 0.5 shard_map.56.packed
  32.6 0.5 collective-permute-done.4.offset_sib
  33.1 0.4 shard_map.57
  33.5 14.8 %all_to_all.10.recv = bf16[4,456,128]{2,1,0:T(8,128)(2,1)S(1)} all-to-all(bf16[4,456,128]{2,1,0:T(8,128)(2,1)S(1)} %shard_map.57), channel_id=1, replica_groups={{0,32,64,96},{16,48,80,112},{128,160,192,224},{144,176,208,240},{256,28..., dimensions={0} | all-to-all | bytes 933888 | tf_op jit(solution)/shard_map/all_to_all | solution.py:327
  48.3 1.0 %shard_map.58 = (bf16[3,2,135,135]{3,2,1,0:T(8,128)(2,1)S(1)}, f32[3,135,128]{2,1,0:T(8,128)S(1)}, bf16[600,128]{1,0:T(8,128)(2,1)S(1)}) custom-call(bf16[4,456,128]{2,1,0:T(8,128)(2,1)S(1)} %all_to_all.10.recv), custom_call_target="tpu_custom_call" | custom-call | tf_op jit(solution)/shard_map/pallas_call | solution.py:262
  49.3 11.1 %all-gather = bf16[2400,128]{1,0:T(8,128)(2,1)S(1)} all-gather(bf16[600,128]{1,0:T(8,128)(2,1)S(1)} %get-tuple-element.22), channel_id=2, replica_groups={{0,128,256,384},{16,144,272,400},{32,160,288,416},{48,176,304,432},{64,..., dimensions={0}, use_global_device_ids=true | all-gather | bytes 768000 | tf_op jit(solution)/shard_map/all_gather | solution.py:338
  60.5 0.9 %shard_map.59 = bf16[4,136,128]{2,1,0:T(8,128)(2,1)S(1)} custom-call(s32[1]{0:T(128)} %bitcast.place, bf16[4,600,128]{2,1,0:T(8,128)(2,1)S(1)} %bitcast.8, bf16[3,2,135,135]{3,2,1,0:T(8,128)(2,1)S(1)} %get-tuple-element.23.prefix, f32[3,135,128]{2,1,0:T(8,128)S(1)} %get-tuple-element.24.shifts), custom_call_target="tpu_custom_call" | custom-call | tf_op jit(solution)/shard_map/pallas_call | solution.py:262
  61.4 11.6 %all_to_all.11.inflow = bf16[4,136,128]{2,1,0:T(8,128)(2,1)S(1)} all-to-all(bf16[4,136,128]{2,1,0:T(8,128)(2,1)S(1)} %shard_map.59), channel_id=1, replica_groups={{0,32,64,96},{16,48,80,112},{128,160,192,224},{144,176,208,240},{256,28..., dimensions={0} | all-to-all | bytes 278528 | tf_op jit(solution)/shard_map/all_to_all | solution.py:345
  73.0 8.9 %collective-permute-start.5 = (bf16[3,136,128]{2,1,0:T(8,128)(2,1)S(1)}, bf16[3,136,128]{2,1,0:T(8,128)(2,1)S(1)}, u32[]{:S(2)}, u32[]{:S(2)}) collective-permute-start(bf16[3,136,128]{2,1,0:T(8,128)(2,1)S(1)} %shard_map.61), channel_id=1, source_target_pairs={{0,16},{16,0},{32,48},{48,32},{64,80},{80,64},{96,112},{112,96},{1... | collective-permute-start | bytes 313352 | tf_op jit(solution)/shard_map/ppermute | solution.py:348
  81.9 0.9 %shard_map.60.half = f32[3,135,128]{2,1,0:T(8,128)S(1)} custom-call(s32[1]{0:T(128)} %bitcast.place, f32[6,136,256]{2,1,0:T(8,128)S(1)} %get-tuple-element.15.transfer, f32[6,135,128]{2,1,0:T(8,128)S(1)} %get-tuple-element.19.offset, f32[3,136,256]{2,1,0:T(8,128)S(1)} %collective-permute-done.3.sib, f32[3,136,128]{2,1,0:T(8,128)S(1)} %collective-permute-done.4.offset_sib, ...), custom_call_target="tpu_custom_call" | custom-call | tf_op jit(solution)/shard_map/pallas_call | solution.py:262
  82.8 0.0 collective-permute-done.5.inflow
  82.9 1.2 %shard_map.62 = f32[810,1,128]{2,1,0:T(1,128)} custom-call(s32[1]{0:T(128)} %bitcast.place, f32[6,136,256]{2,1,0:T(8,128)S(1)} %get-tuple-element.15.transfer, f32[6,135,128]{2,1,0:T(8,128)S(1)} %get-tuple-element.19.offset, f32[3,135,128]{2,1,0:T(8,128)S(1)} %shard_map.60.half, bf16[3,136,128]{2,1,0:T(8,128)(2,1)S(1)} %collective-permute-done.5.inflow), custom_call_target="tpu_custom_call" | custom-call | tf_op jit(solution)/shard_map/pallas_call | solution.py:262
  (1 shorter events, 0.0 us)
Async XLA Ops:
  0.0 4.6 %copy-start = (bf16[1,1,6,135,128]{4,3,2,1,0:T(8,128)(2,1)S(1)}, bf16[1,1,6,135,128]{4,3,2,1,0:T(8,128)(2,1)}, u32[]{:S(2)}) copy-start(bf16[1,1,6,135,128]{4,3,2,1,0:T(8,128)(2,1)} %param.8) | copy-start | bytes 622084
  2.0 30.0 %collective-permute-start.3 = (f32[3,136,256]{2,1,0:T(8,128)S(1)}, f32[3,136,256]{2,1,0:T(8,128)S(1)}, u32[]{:S(2)}, u32[]{:S(2)}) collective-permute-start(f32[3,136,256]{2,1,0:T(8,128)S(1)} %get-tuple-element.20), channel_id=1, source_target_pairs={{0,16},{16,0},{32,48},{48,32},{64,80},{80,64},{96,112},{112,96},{1... | collective-permute-start | bytes 1253384 | tf_op jit(solution)/shard_map/ppermute | solution.py:307
  4.6 11.4 %collective-permute-start = (bf16[6,135,128]{2,1,0:T(8,128)(2,1)S(1)}, bf16[6,135,128]{2,1,0:T(8,128)(2,1)S(1)}, u32[]{:S(2)}, u32[]{:S(2)}) collective-permute-start(bf16[6,135,128]{2,1,0:T(8,128)(2,1)S(1)} %bitcast.12), channel_id=1, source_target_pairs={{16,0},{32,16},{48,32},{64,48},{80,64},{96,80},{112,96},{128,112},... | collective-permute-start | bytes 622088 | tf_op jit(solution)/shard_map/ppermute | solution.py:281
  6.6 9.5 %collective-permute-start.1 = (bf16[6,135,128]{2,1,0:T(8,128)(2,1)S(1)}, bf16[6,135,128]{2,1,0:T(8,128)(2,1)S(1)}, u32[]{:S(2)}, u32[]{:S(2)}) collective-permute-start(bf16[6,135,128]{2,1,0:T(8,128)(2,1)S(1)} %bitcast.13), channel_id=1, source_target_pairs={{0,1},{1,2},{2,3},{3,4},{4,5},{5,6},{6,7},{7,8},{8,9},{9,10},{10,1... | collective-permute-start | bytes 622088 | tf_op jit(solution)/shard_map/ppermute | solution.py:279
  11.0 7.8 %collective-permute-start.2 = (bf16[6,135,128]{2,1,0:T(8,128)(2,1)S(1)}, bf16[6,135,128]{2,1,0:T(8,128)(2,1)S(1)}, u32[]{:S(2)}, u32[]{:S(2)}) collective-permute-start(bf16[6,135,128]{2,1,0:T(8,128)(2,1)S(1)} %bitcast.14), channel_id=1, source_target_pairs={{1,0},{2,1},{3,2},{4,3},{5,4},{6,5},{7,6},{8,7},{9,8},{10,9},{11,1... | collective-permute-start | bytes 622088 | tf_op jit(solution)/shard_map/ppermute | solution.py:280
  19.3 13.8 %collective-permute-start.4 = (f32[3,136,128]{2,1,0:T(8,128)S(1)}, f32[3,136,128]{2,1,0:T(8,128)S(1)}, u32[]{:S(2)}, u32[]{:S(2)}) collective-permute-start(f32[3,136,128]{2,1,0:T(8,128)S(1)} %get-tuple-element.21), channel_id=1, source_target_pairs={{0,16},{16,0},{32,48},{48,32},{64,80},{80,64},{96,112},{112,96},{1... | collective-permute-start | bytes 626696 | tf_op jit(solution)/shard_map/ppermute | solution.py:323
  73.0 9.8 %collective-permute-start.5 = (bf16[3,136,128]{2,1,0:T(8,128)(2,1)S(1)}, bf16[3,136,128]{2,1,0:T(8,128)(2,1)S(1)}, u32[]{:S(2)}, u32[]{:S(2)}) collective-permute-start(bf16[3,136,128]{2,1,0:T(8,128)(2,1)S(1)} %shard_map.61), channel_id=1, source_target_pairs={{0,16},{16,0},{32,48},{48,32},{64,80},{80,64},{96,112},{112,96},{1... | collective-permute-start | bytes 313352 | tf_op jit(solution)/shard_map/ppermute | solution.py:348

commit v6 on v5

--- a/solution.py
+++ b/solution.py
@@ -70,7 +70,7 @@
     return ref[at + (slice(SHIFT, SHIFT + BS),)].astype(F32) + ref[at + (slice(LOW, LOW + BS),)].astype(F32)
 
 
-def local_kernel(place, layers_in, inv_in, c_in, rhs_in, prev_in, inv, last, transfer, send, partial, layers, c0, walls, rhs, prev, sems):
+def local_kernel(place, layers_in, inv_in, c_in, rhs_in, prev_in, inv, last, near, transfer, send, partial, layers, c0, walls, rhs, prev, sems):
     moves = (
         (inv_in, inv),
         (c_in.at[0, 0, 0], c0),
@@ -79,6 +79,7 @@
         (layers_in, layers),
         (c_in.at[4, 0, 0], walls.at[0]),
         (c_in.at[5, 0, 0], walls.at[1]),
+        (c_in.at[1, 0, 0], near),
         (c_in.at[3, 0, 0], last),
     )
     copies = [pltpu.make_async_copy(source, target, sems.at[i]) for i, (source, target) in enumerate(moves)]
@@ -123,16 +124,14 @@
     pl.when(c == 1)(lambda: body(1))
 
 
-def early_kernel(c_in, partial, down, lower, out, c, sems):
-    copies = [pltpu.make_async_copy(c_in.at[1 + i, 0, 0], c.at[i], sems.at[i]) for i in range(2)]
-    for copy in copies:
-        copy.start()
-    copies[0].wait()
-    for s in range(NZ):
-        out[s] = partial[s] - mm(c[0, s], down[s])
-    copies[1].wait()
-    for s in range(NZ):
-        out[s] = out[s] - mm(c[1, s], lower[s])
+def early_kernel(c_in, near, partial, down, lower, out, c, sem):
+    copy = pltpu.make_async_copy(c_in.at[2, 0, 0], c, sem)
+    copy.start()
+    for s in range(NZ):
+        out[s] = partial[s] - mm(near[s], down[s])
+    copy.wait()
+    for s in range(NZ):
+        out[s] = out[s] - mm(c[s], lower[s])
 
 
 def offset_kernel(place, inv, c, partial, upper, out, send):
@@ -282,9 +281,10 @@
 
     anywhere = pl.BlockSpec(memory_space=pl.ANY)
     whole = [pltpu.with_memory_space_constraint(a, pltpu.HBM) for a in (slot_layer, inv, couplings, rhs, prev)]
-    inv, last, transfer, send, partial = pl.pallas_call(
+    inv, last, near, transfer, send, partial = pl.pallas_call(
         local_kernel,
         out_shape=(
+            vmem(NZ, BS, BS, dtype=BF16),
             vmem(NZ, BS, BS, dtype=BF16),
             vmem(NZ, BS, BS, dtype=BF16),
             vmem(NZ, ROWS, 2 * LANE),
@@ -292,14 +292,14 @@
             vmem(NZ, BS, NRHS),
         ),
         in_specs=[SMEM] + [anywhere] * 5,
-        out_specs=(VMEM,) * 5,
+        out_specs=(VMEM,) * 6,
         scratch_shapes=[
             pltpu.SMEM((1, 1, NZ), jnp.int32),
             pltpu.VMEM((NZ, BS, BS), BF16),
             pltpu.VMEM((2, NZ, BS, BS), BF16),
             pltpu.VMEM((NZ, BS, NRHS), BF16),
             pltpu.VMEM((NZ, BS, NRHS), BF16),
-            pltpu.SemaphoreType.DMA((8,)),
+            pltpu.SemaphoreType.DMA((9,)),
         ],
         name="local_kernel",
         compiler_params=PARAMS,
@@ -309,12 +309,13 @@
     partial = pl.pallas_call(
         early_kernel,
         out_shape=vmem(NZ, BS, NRHS),
-        in_specs=[anywhere] + [VMEM] * 3,
+        in_specs=[anywhere] + [VMEM] * 4,
+        input_output_aliases={2: 0},
         out_specs=VMEM,
-        scratch_shapes=[pltpu.VMEM((2, NZ, BS, BS), BF16), pltpu.SemaphoreType.DMA((2,))],
+        scratch_shapes=[pltpu.VMEM((NZ, BS, BS), BF16), pltpu.SemaphoreType.DMA(())],
         name="early_kernel",
         compiler_params=PARAMS,
-    )(whole[2], *(pltpu.with_memory_space_constraint(a, pltpu.VMEM) for a in (partial, down, lower)))
+    )(whole[2], *(pltpu.with_memory_space_constraint(a, pltpu.VMEM) for a in (near, partial, down, lower)))
     offset, send = call(
         offset_kernel,
         (vmem(NZ, BS, NRHS), vmem(HALF, ROWS, NRHS)),

time: 84.4 us -> 84.4 us (level)
  no operation moved by 1% of the time
where the time goes in v6:
time: 84.4 us; the launch traced here: 84 us
  blocking collectives  37.6 us (45%)
  starting transfers between devices  32.5 us (39%)
  Pallas kernels  8.82 us (10%)
  waiting for transfers between devices  4.97 us (6%)
    all_to_all x1, blocking collectives, local(): maps = lax.all_to_all(send, 'sweep', 0, 0, axis_index_groups=RUNS)  14.8 us
    ppermute x1, starting transfers between devices, local(): offset_sib = lax.ppermute(send, 'sweep', swap)  12.8 us
    all_to_all x1, blocking collectives, local(): inflow = lax.all_to_all(back, 'sweep', 0, 0, axis_index_groups=RUNS)  11.6 us
    all_gather x1, blocking collectives, local(): totals = lax.all_gather(total, 'sweep', axis_index_groups=ACROSS)  11.1 us
    ppermute x1, starting transfers between devices, local(): inflow = lax.ppermute(send, 'sweep', swap)  8.89 us
    pallas_call x8, Pallas kernels, call(): pl.pallas_call(kernel, out_shape=outs, in_specs=[SMEM if one else VMEM fo...  5.42 us
    ppermute x1, starting transfers between devices, local(): lax.ppermute(prev, 'span', [(i, (i + 1) % n_span) for i in range(n_span)])  4.41 us
    ppermute x1, waiting for transfers between devices, local(): down = lax.ppermute(prev, 'sweep', [(i + 1, i) for i in range(n_sweep - 1)])  3.15 us
  transfers between devices with their start and end apart: 6, of which 3 were waited for; matrix products, arithmetic and copies ran while one was open for 0% of the time, Pallas kernels for 4%

profile of v6, /device:TPU:31, one launch (start us, length us, event | category | flops | bytes accessed | tf_op | source)
XLA Modules:
  0.0 84.0 jit_solution(17685279057093614423)
XLA Ops:
  0.0 0.0 copy-start
  0.0 2.0 %local_kernel.1 = (bf16[6,135,135]{2,1,0:T(8,128)(2,1)S(1)}, bf16[6,135,135]{2,1,0:T(8,128)(2,1)S(1)}, bf16[6,135,135]{2,1,0:T(8,128)(2,1)S(1)}, f32[6,136,256]{...) custom-call(s32[1]{0:T(128)} %bitcast.place, s32[1,1,6]{2,1,0:T(1,128)} %layers_in.1, ...), custom_call_target="tpu_custom_call" | custom-call | tf_op jit(solution)/shard_map/local_kernel/pallas_call | solution.py:284
  2.0 2.6 %collective-permute-start.3 = (f32[3,136,256]{2,1,0:T(8,128)S(1)}, f32[3,136,256]{2,1,0:T(8,128)S(1)}, u32[]{:S(2)}, u32[]{:S(2)}) collective-permute-start(f32[3,136,256]{2,1,0:T(8,128)S(1)} %get-tuple-element.22), channel_id=1, source_target_pairs={{0,16},{16,0},{32,48},{48,32},{64,80},{80,64},{96,112},{112,96},{1... | collective-permute-start | bytes 1253384 | tf_op jit(solution)/shard_map/ppermute | solution.py:307
  4.6 0.0 copy-done
  4.6 1.9 %collective-permute-start = (bf16[6,135,128]{2,1,0:T(8,128)(2,1)S(1)}, bf16[6,135,128]{2,1,0:T(8,128)(2,1)S(1)}, u32[]{:S(2)}, u32[]{:S(2)}) collective-permute-start(bf16[6,135,128]{2,1,0:T(8,128)(2,1)S(1)} %bitcast.12), channel_id=1, source_target_pairs={{16,0},{32,16},{48,32},{64,48},{80,64},{96,80},{112,96},{128,112},... | collective-permute-start | bytes 622088 | tf_op jit(solution)/shard_map/ppermute | solution.py:280
  6.6 4.4 %collective-permute-start.1 = (bf16[6,135,128]{2,1,0:T(8,128)(2,1)S(1)}, bf16[6,135,128]{2,1,0:T(8,128)(2,1)S(1)}, u32[]{:S(2)}, u32[]{:S(2)}) collective-permute-start(bf16[6,135,128]{2,1,0:T(8,128)(2,1)S(1)} %bitcast.13), channel_id=1, source_target_pairs={{0,1},{1,2},{2,3},{3,4},{4,5},{5,6},{6,7},{7,8},{8,9},{9,10},{10,1... | collective-permute-start | bytes 622088 | tf_op jit(solution)/shard_map/ppermute | solution.py:278
  11.0 1.9 %collective-permute-start.2 = (bf16[6,135,128]{2,1,0:T(8,128)(2,1)S(1)}, bf16[6,135,128]{2,1,0:T(8,128)(2,1)S(1)}, u32[]{:S(2)}, u32[]{:S(2)}) collective-permute-start(bf16[6,135,128]{2,1,0:T(8,128)(2,1)S(1)} %bitcast.14), channel_id=1, source_target_pairs={{1,0},{2,1},{3,2},{4,3},{5,4},{6,5},{7,6},{8,7},{9,8},{10,9},{11,1... | collective-permute-start | bytes 622088 | tf_op jit(solution)/shard_map/ppermute | solution.py:279
  12.9 3.1 %collective-permute-done.down = bf16[6,135,128]{2,1,0:T(8,128)(2,1)S(1)} collective-permute-done((bf16[6,135,128]{2,1,0:T(8,128)(2,1)S(1)}, bf16[6,135,128]{2,1,0:T(8,128)(2,1)S(1)}, u32[]{:S(2)}, u32[]{:S(2)}) %collective-permute-start) | collective-permute-done | bytes 207392 | tf_op jit(solution)/shard_map/ppermute | solution.py:280
  16.1 0.0 collective-permute-done.1.lower
  16.1 1.4 %early_kernel.1.partial = f32[6,135,128]{2,1,0:T(8,128)S(1)} custom-call(bf16[6,1,1,6,135,135]{5,4,3,2,1,0:T(8,128)(2,1)} %c_in.3, bf16[6,135,135]{2,1,0:T(8,128)(2,1)S(1)} %get-tuple-element.19.near, f32[6,135,128]{2,1,0:T(8,128)S(1)} %get-tuple-element.20.partial, ...), custom_call_target="tpu_custom_call", output_to_operand_aliasing={{}: (2, {})} | custom-call | tf_op jit(solution)/shard_map/early_kernel/pallas_call | solution.py:309
  17.4 1.3 %collective-permute-done.2.upper = bf16[6,135,128]{2,1,0:T(8,128)(2,1)S(1)} collective-permute-done((bf16[6,135,128]{2,1,0:T(8,128)(2,1)S(1)}, bf16[6,135,128]{2,1,0:T(8,128)(2,1)S(1)}, u32[]{:S(2)}, u32[]{:S(2)}) %collective-permute-start.2) | collective-permute-done | bytes 207392 | tf_op jit(solution)/shard_map/ppermute | solution.py:279
  18.7 0.5 shard_map.55
  19.3 12.8 %collective-permute-start.4 = (f32[3,136,128]{2,1,0:T(8,128)S(1)}, f32[3,136,128]{2,1,0:T(8,128)S(1)}, u32[]{:S(2)}, u32[]{:S(2)}) collective-permute-start(f32[3,136,128]{2,1,0:T(8,128)S(1)} %get-tuple-element.23), channel_id=1, source_target_pairs={{0,16},{16,0},{32,48},{48,32},{64,80},{80,64},{96,112},{112,96},{1... | collective-permute-start | bytes 626696 | tf_op jit(solution)/shard_map/ppermute | solution.py:324
  32.1 0.0 collective-permute-done.3.sib
  32.1 0.5 shard_map.56.packed
  32.6 0.5 collective-permute-done.4.offset_sib
  33.1 0.4 shard_map.57
  33.5 14.8 %all_to_all.10.recv = bf16[4,456,128]{2,1,0:T(8,128)(2,1)S(1)} all-to-all(bf16[4,456,128]{2,1,0:T(8,128)(2,1)S(1)} %shard_map.57), channel_id=1, replica_groups={{0,32,64,96},{16,48,80,112},{128,160,192,224},{144,176,208,240},{256,28..., dimensions={0} | all-to-all | bytes 933888 | tf_op jit(solution)/shard_map/all_to_all | solution.py:328
  48.3 1.0 %shard_map.58 = (bf16[3,2,135,135]{3,2,1,0:T(8,128)(2,1)S(1)}, f32[3,135,128]{2,1,0:T(8,128)S(1)}, bf16[600,128]{1,0:T(8,128)(2,1)S(1)}) custom-call(bf16[4,456,128]{2,1,0:T(8,128)(2,1)S(1)} %all_to_all.10.recv), custom_call_target="tpu_custom_call" | custom-call | tf_op jit(solution)/shard_map/pallas_call | solution.py:261
  49.4 11.1 %all-gather = bf16[2400,128]{1,0:T(8,128)(2,1)S(1)} all-gather(bf16[600,128]{1,0:T(8,128)(2,1)S(1)} %get-tuple-element.24), channel_id=2, replica_groups={{0,128,256,384},{16,144,272,400},{32,160,288,416},{48,176,304,432},{64,..., dimensions={0}, use_global_device_ids=true | all-gather | bytes 768000 | tf_op jit(solution)/shard_map/all_gather | solution.py:339
  60.5 0.9 %shard_map.59 = bf16[4,136,128]{2,1,0:T(8,128)(2,1)S(1)} custom-call(s32[1]{0:T(128)} %bitcast.place, bf16[4,600,128]{2,1,0:T(8,128)(2,1)S(1)} %bitcast.8, bf16[3,2,135,135]{3,2,1,0:T(8,128)(2,1)S(1)} %get-tuple-element.25.prefix, f32[3,135,128]{2,1,0:T(8,128)S(1)} %get-tuple-element.26.shifts), custom_call_target="tpu_custom_call" | custom-call | tf_op jit(solution)/shard_map/pallas_call | solution.py:261
  61.4 11.6 %all_to_all.11.inflow = bf16[4,136,128]{2,1,0:T(8,128)(2,1)S(1)} all-to-all(bf16[4,136,128]{2,1,0:T(8,128)(2,1)S(1)} %shard_map.59), channel_id=1, replica_groups={{0,32,64,96},{16,48,80,112},{128,160,192,224},{144,176,208,240},{256,28..., dimensions={0} | all-to-all | bytes 278528 | tf_op jit(solution)/shard_map/all_to_all | solution.py:346
  73.0 8.9 %collective-permute-start.5 = (bf16[3,136,128]{2,1,0:T(8,128)(2,1)S(1)}, bf16[3,136,128]{2,1,0:T(8,128)(2,1)S(1)}, u32[]{:S(2)}, u32[]{:S(2)}) collective-permute-start(bf16[3,136,128]{2,1,0:T(8,128)(2,1)S(1)} %shard_map.61), channel_id=1, source_target_pairs={{0,16},{16,0},{32,48},{48,32},{64,80},{80,64},{96,112},{112,96},{1... | collective-permute-start | bytes 313352 | tf_op jit(solution)/shard_map/ppermute | solution.py:349
  81.9 0.9 %shard_map.60.half = f32[3,135,128]{2,1,0:T(8,128)S(1)} custom-call(s32[1]{0:T(128)} %bitcast.place, f32[6,136,256]{2,1,0:T(8,128)S(1)} %get-tuple-element.16.transfer, f32[6,135,128]{2,1,0:T(8,128)S(1)} %get-tuple-element.21.offset, f32[3,136,256]{2,1,0:T(8,128)S(1)} %collective-permute-done.3.sib, f32[3,136,128]{2,1,0:T(8,128)S(1)} %collective-permute-done.4.offset_sib, ...), custom_call_target="tpu_custom_call" | custom-call | tf_op jit(solution)/shard_map/pallas_call | solution.py:261
  82.9 0.0 collective-permute-done.5.inflow
  82.9 1.2 %shard_map.62 = f32[810,1,128]{2,1,0:T(1,128)} custom-call(s32[1]{0:T(128)} %bitcast.place, f32[6,136,256]{2,1,0:T(8,128)S(1)} %get-tuple-element.16.transfer, f32[6,135,128]{2,1,0:T(8,128)S(1)} %get-tuple-element.21.offset, f32[3,135,128]{2,1,0:T(8,128)S(1)} %shard_map.60.half, bf16[3,136,128]{2,1,0:T(8,128)(2,1)S(1)} %collective-permute-done.5.inflow), custom_call_target="tpu_custom_call" | custom-call | tf_op jit(solution)/shard_map/pallas_call | solution.py:261
  (1 shorter events, 0.0 us)
Async XLA Ops:
  0.0 4.6 %copy-start = (bf16[1,1,6,135,128]{4,3,2,1,0:T(8,128)(2,1)S(1)}, bf16[1,1,6,135,128]{4,3,2,1,0:T(8,128)(2,1)}, u32[]{:S(2)}) copy-start(bf16[1,1,6,135,128]{4,3,2,1,0:T(8,128)(2,1)} %param.8) | copy-start | bytes 622084
  2.0 30.0 %collective-permute-start.3 = (f32[3,136,256]{2,1,0:T(8,128)S(1)}, f32[3,136,256]{2,1,0:T(8,128)S(1)}, u32[]{:S(2)}, u32[]{:S(2)}) collective-permute-start(f32[3,136,256]{2,1,0:T(8,128)S(1)} %get-tuple-element.22), channel_id=1, source_target_pairs={{0,16},{16,0},{32,48},{48,32},{64,80},{80,64},{96,112},{112,96},{1... | collective-permute-start | bytes 1253384 | tf_op jit(solution)/shard_map/ppermute | solution.py:307
  4.6 11.4 %collective-permute-start = (bf16[6,135,128]{2,1,0:T(8,128)(2,1)S(1)}, bf16[6,135,128]{2,1,0:T(8,128)(2,1)S(1)}, u32[]{:S(2)}, u32[]{:S(2)}) collective-permute-start(bf16[6,135,128]{2,1,0:T(8,128)(2,1)S(1)} %bitcast.12), channel_id=1, source_target_pairs={{16,0},{32,16},{48,32},{64,48},{80,64},{96,80},{112,96},{128,112},... | collective-permute-start | bytes 622088 | tf_op jit(solution)/shard_map/ppermute | solution.py:280
  6.6 9.5 %collective-permute-start.1 = (bf16[6,135,128]{2,1,0:T(8,128)(2,1)S(1)}, bf16[6,135,128]{2,1,0:T(8,128)(2,1)S(1)}, u32[]{:S(2)}, u32[]{:S(2)}) collective-permute-start(bf16[6,135,128]{2,1,0:T(8,128)(2,1)S(1)} %bitcast.13), channel_id=1, source_target_pairs={{0,1},{1,2},{2,3},{3,4},{4,5},{5,6},{6,7},{7,8},{8,9},{9,10},{10,1... | collective-permute-start | bytes 622088 | tf_op jit(solution)/shard_map/ppermute | solution.py:278
  11.0 7.8 %collective-permute-start.2 = (bf16[6,135,128]{2,1,0:T(8,128)(2,1)S(1)}, bf16[6,135,128]{2,1,0:T(8,128)(2,1)S(1)}, u32[]{:S(2)}, u32[]{:S(2)}) collective-permute-start(bf16[6,135,128]{2,1,0:T(8,128)(2,1)S(1)} %bitcast.14), channel_id=1, source_target_pairs={{1,0},{2,1},{3,2},{4,3},{5,4},{6,5},{7,6},{8,7},{9,8},{10,9},{11,1... | collective-permute-start | bytes 622088 | tf_op jit(solution)/shard_map/ppermute | solution.py:279
  19.3 13.8 %collective-permute-start.4 = (f32[3,136,128]{2,1,0:T(8,128)S(1)}, f32[3,136,128]{2,1,0:T(8,128)S(1)}, u32[]{:S(2)}, u32[]{:S(2)}) collective-permute-start(f32[3,136,128]{2,1,0:T(8,128)S(1)} %get-tuple-element.23), channel_id=1, source_target_pairs={{0,16},{16,0},{32,48},{48,32},{64,80},{80,64},{96,112},{112,96},{1... | collective-permute-start | bytes 626696 | tf_op jit(solution)/shard_map/ppermute | solution.py:324
  73.0 9.8 %collective-permute-start.5 = (bf16[3,136,128]{2,1,0:T(8,128)(2,1)S(1)}, bf16[3,136,128]{2,1,0:T(8,128)(2,1)S(1)}, u32[]{:S(2)}, u32[]{:S(2)}) collective-permute-start(bf16[3,136,128]{2,1,0:T(8,128)(2,1)S(1)} %shard_map.61), channel_id=1, source_target_pairs={{0,16},{16,0},{32,48},{48,32},{64,80},{80,64},{96,112},{112,96},{1... | collective-permute-start | bytes 313352 | tf_op jit(solution)/shard_map/ppermute | solution.py:349
